TPU v7x, 128 devices: a whole 4x4x4 slice. The times are simulated.
128 devices in a mesh: box: 4 (over z_hi, core), dir: 32 (over x, z_lo, y).
Axes of the slice: x: 4, y: 4, z: 4 (z_hi: 2, z_lo: 2; z = z_hi * 2 + z_lo), core: 2. Of those that a mesh axis runs over, the one named last changes fastest.
Arguments:
- fine_pattern: bfloat16 [512, 2, 16, 8192], P(('box', 'dir')), may hold values from -6 to 6
- fine_interp: bfloat16 [32, 384, 896], P('dir'), may hold values from -0.3125 to 0.3125
- mid_interp: bfloat16 [32, 1024, 3328], P('dir'), may hold values from -0.1875 to 0.1875
- fine_angle: float32 [8, 28672], P(None, 'dir'), may hold values from -3.140625 to 3.140625
- top_angle: float32 [8, 106496], P(None, 'dir'), may hold values from -3.140625 to 3.140625
- translator: bfloat16 [64, 2, 106496], P(None, None, 'dir'), may hold values from -1 to 1
- fine_position: int32 [512], replicated, may hold values from 0 to 7
- mid_position: int32 [128], replicated, may hold values from 0 to 7
- fine_parent: int32 [512], replicated, may hold values from 0 to 127, as said below
- mid_parent: int32 [128], replicated, may hold values from 0 to 31, as said below
- pair_target: int32 [256], replicated, may hold values from 0 to 31
- pair_source: int32 [256], replicated, may hold values from 0 to 31
- pair_kind: int32 [256], replicated, may hold values from 0 to 63
Outputs:
- top_incoming: float32 [32, 2, 16, 106496], P('box', None, None, 'dir')
- mid_incoming: float32 [128, 2, 16, 28672], P('box', None, None, 'dir')
Inputs may be any that keep to these rules, and one draw needn't show every extreme that they name: `fine_parent`: for every k, the fine boxes k * 128 to (k + 1) * 128 - 1 have their parents among the middle boxes k * 32 to (k + 1) * 32 - 1, and every middle box has exactly 4 children. `mid_parent`: for every k, the middle boxes k * 32 to (k + 1) * 32 - 1 have their parents among the top boxes k * 8 to (k + 1) * 8 - 1, and every top box has exactly 4 children.
All inputs are finite; a program needn't handle non-finite values.
Results may differ from a plain program's by a relative error of at most 0.0072.
Values may be sent and summed in bfloat16 or wider, within the bound.
No kernel may reach another device: no remote copies, remote signals or barrier semaphores. Data moves between devices by JAX's collectives and lax.ppermute only.
A program may use at most 128 MiB of HBM per device.

v0:
```python
import jax
import jax.numpy as jnp
from jax import lax
from jax.sharding import PartitionSpec as P

FS = 256
MS = 896
TS = 3328
HALO = 64


def extended(cells, sides, width):
    for axis, dim in sides:
        count = lax.axis_size(axis)
        head = lax.slice_in_dim(cells, 0, width, axis=dim)
        tail = lax.slice_in_dim(cells, cells.shape[dim] - width, cells.shape[dim], axis=dim)
        cells = jnp.concatenate(
            [
                lax.ppermute(tail, axis, [(i, (i + 1) % count) for i in range(count)]),
                cells,
                lax.ppermute(head, axis, [((i + 1) % count, i) for i in range(count)]),
            ],
            axis=dim,
        )
    return cells


def from_behind(shard, axis, by):
    peers = lax.axis_size(axis)
    return lax.ppermute(shard, axis, [(i, (i + by) % peers) for i in range(peers)])


def settle(values):
    return lax.optimization_barrier(values.astype(jnp.bfloat16))


def interpolate(widened, matrices):
    results = jnp.einsum("bcrk,kn->bcrn", widened, matrices[0], preferred_element_type=jnp.float32)
    return results


def turn(pattern, angle_table, positions, direction_sign):
    angles = angle_table[positions]
    cosine = jnp.cos(angles)[:, None, :]
    sine = direction_sign * jnp.sin(angles)[:, None, :]
    real_part = pattern[:, 0].astype(jnp.float32)
    imag_part = pattern[:, 1].astype(jnp.float32)
    return jnp.stack(
        [cosine * real_part - sine * imag_part, sine * real_part + cosine * imag_part], axis=1
    )


def lift_to_parents(coarse, angle_table, positions, parents, base, parent_count):
    turned = turn(coarse, angle_table, positions, 1.0)
    children = turned.shape[0]
    member = (
        (parents - base)[None, :] == jnp.arange(parent_count, dtype=jnp.int32)[:, None]
    ).astype(jnp.float32)
    summed = jnp.dot(member, turned.reshape(children, -1), precision=lax.Precision.HIGHEST)
    return settle(summed.reshape((parent_count,) + turned.shape[1:]))


def pick_parents(rounded, parents, base):
    parent_count = rounded.shape[0]
    member = (
        (parents - base)[:, None] == jnp.arange(parent_count, dtype=jnp.int32)[None, :]
    ).astype(jnp.bfloat16)
    picked = jnp.dot(member, rounded.reshape(parent_count, -1), preferred_element_type=jnp.float32)
    return picked.reshape((parents.shape[0],) + rounded.shape[1:])


def pair_counts(
    pair_target, pair_source, pair_kind, target_base, target_count, source_count, kind_count
):
    inside = (pair_target >= target_base) & (pair_target < target_base + target_count)
    slot_index = jnp.where(inside, (pair_target - target_base) * source_count + pair_source, -1)
    onehot_pair = (
        slot_index[:, None] == jnp.arange(target_count * source_count, dtype=jnp.int32)[None, :]
    ).astype(jnp.float32)
    onehot_kind = (pair_kind[:, None] == jnp.arange(kind_count, dtype=jnp.int32)[None, :]).astype(
        jnp.float32
    )
    return jnp.dot(onehot_pair.T, onehot_kind, precision=lax.Precision.HIGHEST).astype(jnp.bfloat16)


def translate(coupling, sources):
    targets = coupling.shape[0]
    initial = jnp.zeros((targets, 2) + sources.shape[2:], jnp.float32)

    def add_source(source_row, running):
        operator_row = lax.dynamic_index_in_dim(coupling, source_row, 1, keepdims=False).astype(
            jnp.float32
        )
        source_field = lax.dynamic_index_in_dim(sources, source_row, 0, keepdims=False).astype(
            jnp.float32
        )
        op_real = operator_row[:, 0][:, None, :]
        op_imag = operator_row[:, 1][:, None, :]
        src_real = source_field[0][None]
        src_imag = source_field[1][None]
        product = jnp.stack(
            [op_real * src_real - op_imag * src_imag, op_real * src_imag + op_imag * src_real],
            axis=1,
        )
        return running + product

    return lax.fori_loop(0, sources.shape[0], add_source, initial)


def per_device(
    fine_pattern,
    fine_interp,
    mid_interp,
    fine_angle,
    top_angle,
    translator,
    fine_position,
    mid_position,
    fine_parent,
    mid_parent,
    pair_target,
    pair_source,
    pair_kind,
):
    box_index = lax.axis_index("box")
    dir_count = lax.axis_size("dir")
    box_count = lax.axis_size("box")
    fine_local = fine_pattern.shape[0]
    columns = fine_pattern.shape[2]
    fine_group = fine_local * dir_count
    mid_group = fine_group // 4
    top_group = fine_group // 16
    top_boxes = top_group * box_count
    sectors_here = fine_interp.shape[0]
    fine_block = sectors_here * FS
    mid_block = sectors_here * MS
    top_block = sectors_here * TS
    kind_count = translator.shape[0]
    shape = (fine_local, 2, columns, dir_count, fine_block)
    blocks = fine_pattern.reshape(shape)
    leading = jnp.roll(fine_pattern, HALO, axis=3).reshape(shape)[..., :HALO]
    trailing = jnp.roll(fine_pattern, -HALO, axis=3).reshape(shape)[..., fine_block - HALO :]
    rimmed = jnp.concatenate([leading, blocks, trailing], axis=4)
    arrived = lax.all_to_all(rimmed, "dir", split_axis=3, concat_axis=0, tiled=True)
    widened = arrived.reshape(fine_group, 2, columns, fine_block + 2 * HALO)
    coarse_fine = settle(interpolate(widened, fine_interp))
    fine_positions = lax.dynamic_slice_in_dim(fine_position, box_index * fine_group, fine_group)
    fine_parents = lax.dynamic_slice_in_dim(fine_parent, box_index * fine_group, fine_group)
    mid_pattern = lift_to_parents(
        coarse_fine, fine_angle, fine_positions, fine_parents, box_index * mid_group, mid_group
    )
    widened_mid = extended(mid_pattern, (("dir", 3),), HALO)
    coarse_mid = settle(interpolate(widened_mid, mid_interp))
    mid_positions = lax.dynamic_slice_in_dim(mid_position, box_index * mid_group, mid_group)
    mid_parents = lax.dynamic_slice_in_dim(mid_parent, box_index * mid_group, mid_group)
    top_pattern = lift_to_parents(
        coarse_mid, top_angle, mid_positions, mid_parents, box_index * top_group, top_group
    )
    counts = pair_counts(
        pair_target, pair_source, pair_kind, box_index * top_group, top_group, top_boxes, kind_count
    )
    coupling = settle(
        jnp.dot(
            counts,
            translator.reshape(kind_count, 2 * top_block),
            preferred_element_type=jnp.float32,
        ).reshape(top_group, top_boxes, 2, top_block)
    )
    top_incoming = translate(coupling, lax.all_gather(top_pattern, "box", axis=0, tiled=True))
    top_rounded = settle(top_incoming)
    chosen = pick_parents(top_rounded, mid_parents, box_index * top_group)
    spread = settle(turn(chosen, top_angle, mid_positions, -1.0))
    pieces = jnp.einsum("bcrn,kn->bcrk", spread, mid_interp[0], preferred_element_type=jnp.float32)
    central = pieces[..., HALO : HALO + mid_block]
    from_below = from_behind(pieces[..., HALO + mid_block :].astype(jnp.bfloat16), "dir", 1).astype(
        jnp.float32
    )
    from_above = from_behind(pieces[..., :HALO].astype(jnp.bfloat16), "dir", -1).astype(jnp.float32)
    middle_zeros = jnp.zeros(central.shape[:3] + (mid_block - 2 * HALO,), jnp.float32)
    correction = jnp.concatenate([from_below, middle_zeros, from_above], axis=3)
    return (top_incoming, central + correction)


def solution(mesh):
    placed = (
        P(("box", "dir"), None, None, None),
        P("dir", None, None),
        P("dir", None, None),
        P(None, "dir"),
        P(None, "dir"),
        P(None, None, "dir"),
        P(),
        P(),
        P(),
        P(),
        P(),
        P(),
        P(),
    )
    return jax.shard_map(
        per_device,
        mesh=mesh,
        in_specs=placed,
        out_specs=(P("box", None, None, "dir"), P("box", None, None, "dir")),
        check_vma=False,
    )
```

profile of v0, /device:TPU:1, one launch (start us, length us, event | category | flops | bytes accessed | tf_op | source)
XLA Modules:
  0.0 532.9 jit_solution(17719938760731765016)
XLA Ops:
  16.1 4.1 copy.48
  20.2 9.5 %all-to-all-start = ((bf16[4,2,16,32,384]{4,0,2,1,3:T(4,128)(2,1)}), bf16[4,2,16,32,384]{4,0,2,1,3:T(4,128)(2,1)}, u32[]{:S(2)}, u32[]{:S(2)}) async-start(bf16[4,2,16,32,384]{4,0,2,1,3:T(4,128)(2,1)} %copy.48), calls=%async_computation | async-start | bytes 6291456 | tf_op jit(solution)/shard_map/all_to_all | solution.py:144
  34.6 36.0 %all-to-all-done = bf16[4,2,16,32,384]{4,0,2,1,3:T(4,128)(2,1)} async-done(((bf16[4,2,16,32,384]{4,0,2,1,3:T(4,128)(2,1)}), bf16[4,2,16,32,384]{4,0,2,1,3:T(4,128)(2,1)}, u32[]{:S(2)}, u32[]{:S(2)}) %all-to-all-start) | async-done | bytes 3145760 | tf_op jit(solution)/shard_map/all_to_all | solution.py:144
  70.6 5.2 copy.49
  75.8 5.9 %reshape.88 = bf16[128,2,16,384]{3,0,2,1:T(8,128)(2,1)} reshape(bf16[32,4,2,16,1,384]{5,1,0,3,2,4:T(4,128)(2,1)} %copy.49) | data formatting | bytes 6291456 | tf_op jit(solution)/shard_map/reshape | solution.py:145
  81.7 6.6 %convolution_convert_fusion.2 = bf16[128,2,16,896]{3,0,2,1:T(8,128)(2,1)S(1)} fusion(bf16[128,2,16,384]{3,0,2,1:T(8,128)(2,1)} %reshape.88, bf16[1,384,896]{2,1,0:T(8,128)(2,1)S(1)} %copy-done), kind=kOutput, calls=%fused_computation.38 | convolution fusion | flops 2822242304 | bytes 11173888 | tf_op jit(solution)/shard_map/bcrk,kn->bcrn/dot_general | solution.py:38
  88.4 6.4 %fusion.4 = (f32[128,1,16,896]{3,0,2,1:T(8,128)}, f32[128,1,16,896]{3,0,2,1:T(8,128)}) fusion(f32[128,896]{1,0:T(8,128)S(1)} %get-tuple-element.144, f32[128,896]{1,0:T(8,128)S(1)} %get-tuple-element.143, bf16[128,2,16,896]{3,0,2,1:T(8,128)(2,1)S(1)} %convolution_convert_fusion.2), kind=kLoop, calls=%fused_computation.26 | loop fusion | flops 14680064 | bytes 22937600 | tf_op jit(solution)/shard_map/sub | solution.py:49
  94.7 12.0 %pad_maximum_fusion = f32[128,2,16,896]{3,0,2,1:T(8,128)} fusion(f32[128,1,16,896]{3,0,2,1:T(8,128)} %get-tuple-element.132, f32[128,1,16,896]{3,0,2,1:T(8,128)} %get-tuple-element.131), kind=kLoop, calls=%fused_computation.11 | loop fusion | flops 3670016 | bytes 29360128 | tf_op jit(solution)/shard_map/stack | solution.py:48
  106.7 16.7 %copy.50 = f32[128,2,16,896]{0,3,2,1:T(8,128)} copy(f32[128,2,16,896]{3,0,2,1:T(8,128)} %pad_maximum_fusion) | data formatting | bytes 29360128 | tf_op jit(solution)/shard_map/stack | solution.py:48
  123.4 11.4 %fusion.15 = bf16[32,2,16,896]{3,0,2,1:T(8,128)(2,1)S(1)} fusion(f32[128,2,16,896]{0,3,2,1:T(8,128)} %copy.50, s32[128]{0:T(128)S(1)} %get-tuple-element.152), kind=kOutput, calls=%fused_computation.45 | convolution fusion | flops 1410207744 | bytes 16515584 | tf_op jit(solution)/shard_map/dot_general | solution.py:59
  145.6 9.4 %convolution_convert_fusion = bf16[32,2,16,3328]{3,2,1,0:T(8,128)(2,1)S(1)} fusion(bf16[1,1024,3328]{2,1,0:T(8,128)(2,1)S(1)} %bitcast.132, bf16[32,2,16,1024]{3,0,2,1:T(8,128)(2,1)S(1)} %pad_maximum_fusion.6), kind=kOutput, calls=%fused_computation.25 | convolution fusion | flops 6982729728 | bytes 15728640 | tf_op jit(solution)/shard_map/bcrk,kn->bcrn/dot_general | solution.py:38
  154.9 6.0 %fusion.6 = (f32[32,1,16,3328]{3,2,1,0:T(8,128)}, f32[32,1,16,3328]{3,2,1,0:T(8,128)}) fusion(f32[32,3328]{1,0:T(8,128)S(1)} %get-tuple-element.146, f32[32,3328]{1,0:T(8,128)S(1)} %get-tuple-element.145, bf16[32,2,16,3328]{3,2,1,0:T(8,128)(2,1)S(1)} %convolution_convert_fusion), kind=kLoop, calls=%fused_computation.28 | loop fusion | flops 13631488 | bytes 21299200 | tf_op jit(solution)/shard_map/sub | solution.py:49
  161.0 11.0 %fusion.40 = f32[2,16,3328,32]{2,1,0,3:T(8,128)} fusion(f32[32,1,16,3328]{3,2,1,0:T(8,128)} %get-tuple-element.134, f32[32,1,16,3328]{3,2,1,0:T(8,128)} %get-tuple-element.133), kind=kLoop, calls=%fused_computation.80 | loop fusion | flops 3407872 | bytes 27262976 | tf_op jit(solution)/shard_map/dot_general | solution.py:59
  172.0 17.9 %fusion.11 = bf16[8,2,16,3328]{3,0,2,1:T(8,128)(2,1)} fusion(f32[2,16,3328,32]{2,1,0,3:T(8,128)} %fusion.40, s32[32]{0:T(128)S(1)} %copy-done.9), kind=kOutput, calls=%fused_computation.37 | convolution fusion | flops 328007936 | bytes 15335552 | tf_op jit(solution)/shard_map/dot_general | solution.py:59
  195.8 54.1 %all-gather.2.cloned.1.call-done = bf16[32,2,16,3328]{3,0,2,1:T(8,128)(2,1)} async-done(((bf16[8,2,16,3328]{3,0,2,1:T(8,128)(2,1)}), bf16[32,2,16,3328]{3,0,2,1:T(8,128)(2,1)}) %all-gather.2.cloned.1.call-update) | async-done | bytes 6815760 | tf_op jit(solution)/shard_map/all_gather | solution.py:169
  249.9 9.4 %copy.54 = bf16[32,2,16,3328]{3,2,1,0:T(8,128)(2,1)} copy(bf16[32,2,16,3328]{3,0,2,1:T(8,128)(2,1)} %all-gather.2.cloned.1.call-done) | data formatting | bytes 13631488
  259.4 205.8 %while.14 = (s32[]{:T(128)}, f32[8,2,16,3328]{3,2,1,0:T(8,128)}, bf16[8,32,2,3328]{3,0,2,1:T(8,128)(2,1)}, bf16[32,2,16,3328]{3,2,1,0:T(8,128)(2,1)}, s32[]{:T(128)}, /*index=5*/s32[]{:T(128)}) while((s32[]{:T(128)}, f32[8,2,16,3328]{3,2,1,0:T(8,128)}, bf16[8,32,2,3328]{3,0,2,1:T(8,128)(2,1)}, bf16[32,2,16,3328]{3,2,1,0:T(8,128)(2,1)}, ...), condition=%wide.region_1.2_spmd.clone, body=%wide.region_0.1_spmd.clone.sunk | while | flops 5271555 | bytes 16506967 | solution.py:107
  266.3 4.1 maximum_add_fusion.2
  272.8 4.1 maximum_add_fusion.2
  279.3 4.1 maximum_add_fusion.2
  285.8 4.1 maximum_add_fusion.2
  292.3 4.1 maximum_add_fusion.2
  298.8 4.1 maximum_add_fusion.2
  305.3 4.1 maximum_add_fusion.2
  311.8 4.1 maximum_add_fusion.2
  318.3 4.1 maximum_add_fusion.2
  331.2 4.1 maximum_add_fusion.2
  337.7 4.1 maximum_add_fusion.2
  344.2 4.1 maximum_add_fusion.2
  350.7 4.1 maximum_add_fusion.2
  357.2 4.1 maximum_add_fusion.2
  363.7 4.1 maximum_add_fusion.2
  370.2 4.1 maximum_add_fusion.2
  376.7 4.1 maximum_add_fusion.2
  389.7 4.1 maximum_add_fusion.2
  396.2 4.1 maximum_add_fusion.2
  402.7 4.1 maximum_add_fusion.2
  409.2 4.1 maximum_add_fusion.2
  415.7 4.1 maximum_add_fusion.2
  422.2 4.1 maximum_add_fusion.2
  428.6 4.1 maximum_add_fusion.2
  435.1 4.1 maximum_add_fusion.2
  468.3 5.9 %fusion.28 = f32[32,2,16,3328]{3,0,2,1:T(8,128)} fusion(bf16[2,16,3328,8]{2,3,1,0:T(8,128)(2,1)S(1)} %bitcast.125, s32[32]{0:T(128)S(1)} %copy-done.9), kind=kOutput, calls=%fused_computation.64 | convolution fusion | flops 54526208 | bytes 15335552 | tf_op jit(solution)/shard_map/dot_general | solution.py:68
  474.2 11.4 %fusion.32 = (f32[32,1,16,3328]{3,0,2,1:T(8,128)}, f32[32,1,16,3328]{3,0,2,1:T(8,128)}) fusion(f32[32,2,16,3328]{3,0,2,1:T(8,128)} %fusion.28), kind=kLoop, calls=%fused_computation.72 | loop fusion | bytes 27262976 | tf_op jit(solution)/shard_map/slice | solution.py:46
  485.6 14.7 %subtract_convert_fusion = (bf16[32,1,16,3328]{3,2,1,0:T(8,128)(2,1)S(1)}, bf16[32,1,16,3328]{3,2,1,0:T(8,128)(2,1)S(1)}) fusion(f32[32,1,16,3328]{3,0,2,1:T(8,128)} %get-tuple-element.130, f32[32,1,16,3328]{3,0,2,1:T(8,128)} %get-tuple-element.129, f32[32,3328]{1,0:T(8,128)S(1)} %copy-done.7, f32[32,3328]{1,0:T(8,128)S(1)} %copy-done.6), kind=kLoop, calls=%fused_computation.35 | loop fusion | flops 13631488 | bytes 21299200 | tf_op jit(solution)/shard_map/convert.3
  501.0 9.4 %fusion.39 = (bf16[32,2,16,1024]{3,2,1,0:T(8,128)(2,1)S(1)}, f32[32,2,16,1024]{3,2,1,0:T(8,128)S(1)}) fusion(bf16[32,2,16,3328]{3,2,1,0:T(8,128)(2,1)S(1)} %pad_maximum_fusion.2, bf16[1,1024,3328]{2,1,0:T(8,128)(2,1)} %param.17), kind=kOutput, calls=%fused_computation.79 | convolution fusion | flops 6980370432 | bytes 19922944 | tf_op jit(solution)/shard_map/bcrn,kn->bcrk/dot_general | solution.py:173
  511.9 4.5 collective-permute-start.3
  516.4 6.1 %collective-permute-done.2 = bf16[32,2,16,64]{3,2,1,0:T(8,128)(2,1)S(1)} collective-permute-done((bf16[32,2,16,64]{3,2,1,0:T(8,128)(2,1)S(1)}, bf16[32,2,16,64]{3,2,1,0:T(8,128)(2,1)S(1)}, u32[]{:S(2)}, u32[]{:S(2)}) %collective-permute-start.2) | collective-permute-done | bytes 131104 | tf_op jit(solution)/shard_map/ppermute | solution.py:30
  (245 shorter events, 141.3 us)
Async XLA Ops:
  7.2 74.6 %copy-start = (bf16[1,384,896]{2,1,0:T(8,128)(2,1)S(1)}, bf16[1,384,896]{2,1,0:T(8,128)(2,1)}, u32[]{:S(2)}) copy-start(bf16[1,384,896]{2,1,0:T(8,128)(2,1)} %param.16) | copy-start | bytes 2064388
  7.2 3.2 copy-start.4
  20.2 10.5 %copy-start.2 = (f32[8,896]{1,0:T(8,128)S(1)}, f32[8,896]{1,0:T(8,128)}, u32[]{:S(2)}) copy-start(f32[8,896]{1,0:T(8,128)} %param.18) | copy-start | bytes 86020
  20.2 11.4 %copy-start.12 = (s32[128]{0:T(128)S(1)}, s32[128]{0:T(128)}, u32[]{:S(2)}) copy-start(s32[128]{0:T(128)} %param.22) | copy-start | bytes 1540
  20.2 11.4 %copy-start.13 = (s32[128]{0:T(128)S(1)}, s32[128]{0:T(128)}, u32[]{:S(2)}) copy-start(s32[128]{0:T(128)} %param.24) | copy-start | bytes 1540
  20.2 12.1 %copy-start.3 = (f32[8,3328]{1,0:T(8,128)S(1)}, f32[8,3328]{1,0:T(8,128)}, u32[]{:S(2)}) copy-start(f32[8,3328]{1,0:T(8,128)} %param.19) | copy-start | bytes 319492
  20.2 50.4 %all-to-all-start = ((bf16[4,2,16,32,384]{4,0,2,1,3:T(4,128)(2,1)}), bf16[4,2,16,32,384]{4,0,2,1,3:T(4,128)(2,1)}, u32[]{:S(2)}, u32[]{:S(2)}) async-start(bf16[4,2,16,32,384]{4,0,2,1,3:T(4,128)(2,1)} %copy.48), calls=%async_computation | async-start | bytes 6291456 | tf_op jit(solution)/shard_map/all_to_all | solution.py:144
  29.7 220.3 %all-gather.2.cloned.1.call-start = ((), (), s32[]{:S(2)}) async-start(), calls=%async_computation.1 | async-start | bytes 8519680 | tf_op jit(solution)/shard_map/all_gather | solution.py:169
  123.4 22.2 %slice-start = ((s8[6815744]{0:T(1024)(128)(4,1)}), s8[4194304]{0:T(1024)(128)(4,1)S(1)}, s32[]{:S(2)}) async-start(s8[6815744]{0:T(1024)(128)(4,1)} %bitcast.131), calls=%async_computation.2 | async-start | bytes 8388608
  123.4 22.2 %slice-start.1 = ((s8[6815744]{0:T(1024)(128)(4,1)}), s8[2621440]{0:T(1024)(128)(4,1)S(1)}, s32[]{:S(2)}) async-start(s8[6815744]{0:T(1024)(128)(4,1)} %bitcast.131), calls=%async_computation.3 | async-start | bytes 5242880
  134.9 9.5 %collective-permute-start = (bf16[32,2,16,64]{3,0,2,1:T(8,128)(2,1)S(1)}, bf16[32,2,16,64]{3,0,2,1:T(8,128)(2,1)S(1)}, u32[]{:S(2)}, u32[]{:S(2)}) collective-permute-start(bf16[32,2,16,64]{3,0,2,1:T(8,128)(2,1)S(1)} %get-tuple-element.141), channel_id=1, source_target_pairs={{0,1},{1,2},{2,3},{3,4},{4,5},{5,6},{6,7},{7,8},{8,9},{9,10},{10,1... | collective-permute-start | bytes 393224 | tf_op jit(solution)/shard_map/ppermute | solution.py:19
  137.7 6.6 %collective-permute-start.1 = (bf16[32,2,16,64]{3,0,2,1:T(8,128)(2,1)S(1)}, bf16[32,2,16,64]{3,0,2,1:T(8,128)(2,1)S(1)}, u32[]{:S(2)}, u32[]{:S(2)}) collective-permute-start(bf16[32,2,16,64]{3,0,2,1:T(8,128)(2,1)S(1)} %get-tuple-element.142), channel_id=1, source_target_pairs={{1,0},{2,1},{3,2},{4,3},{5,4},{6,5},{7,6},{8,7},{9,8},{10,9},{11,1... | collective-permute-start | bytes 393224 | tf_op jit(solution)/shard_map/ppermute | solution.py:21
  142.5 12.4 %copy-start.5 = (f32[32,3328]{1,0:T(8,128)}, f32[32,3328]{1,0:T(8,128)S(1)}, u32[]{:S(2)}) copy-start(f32[32,3328]{1,0:T(8,128)S(1)} %get-tuple-element.145) | copy-start | bytes 1277956
  161.0 11.0 %copy-start.9 = (s32[32]{0:T(128)S(1)}, s32[32]{0:T(128)}, u32[]{:S(2)}) copy-start(s32[32]{0:T(128)} %get-tuple-element.150) | copy-start | bytes 388
  171.9 18.0 %copy-start.10 = (s32[256]{0:T(256)S(1)}, s32[256]{0:T(256)}, u32[]{:S(2)}) copy-start(s32[256]{0:T(256)} %param.25) | copy-start | bytes 3076
  171.9 18.0 %copy-start.11 = (s32[256]{0:T(256)S(1)}, s32[256]{0:T(256)}, u32[]{:S(2)}) copy-start(s32[256]{0:T(256)} %param.26) | copy-start | bytes 3076
  171.9 18.0 %copy-start.14 = (s32[256]{0:T(256)S(1)}, s32[256]{0:T(256)}, u32[]{:S(2)}) copy-start(s32[256]{0:T(256)} %param.27) | copy-start | bytes 3076
  171.9 18.4 %copy-start.8 = (bf16[64,2,3328]{2,1,0:T(2,128)(2,1)S(1)}, bf16[64,2,3328]{2,1,0:T(2,128)(2,1)}, u32[]{:S(2)}) copy-start(bf16[64,2,3328]{2,1,0:T(2,128)(2,1)} %param.20) | copy-start | bytes 2555908
  474.2 11.4 %copy-start.6 = (f32[32,3328]{1,0:T(8,128)S(1)}, f32[32,3328]{1,0:T(8,128)}, u32[]{:S(2)}) copy-start(f32[32,3328]{1,0:T(8,128)} %copy-done.5) | copy-start | bytes 1277956
  474.2 11.4 %copy-start.7 = (f32[32,3328]{1,0:T(8,128)S(1)}, f32[32,3328]{1,0:T(8,128)}, u32[]{:S(2)}) copy-start(f32[32,3328]{1,0:T(8,128)} %broadcast_multiply_fusion) | copy-start | bytes 1277956
  510.6 11.9 %collective-permute-start.2 = (bf16[32,2,16,64]{3,2,1,0:T(8,128)(2,1)S(1)}, bf16[32,2,16,64]{3,2,1,0:T(8,128)(2,1)S(1)}, u32[]{:S(2)}, u32[]{:S(2)}) collective-permute-start(bf16[32,2,16,64]{3,2,1,0:T(8,128)(2,1)S(1)} %get-tuple-element.135), channel_id=1, source_target_pairs={{0,1},{1,2},{2,3},{3,4},{4,5},{5,6},{6,7},{7,8},{8,9},{9,10},{10,1... | collective-permute-start | bytes 393224 | tf_op jit(solution)/shard_map/ppermute | solution.py:30
  511.9 10.7 %collective-permute-start.3 = (bf16[32,2,16,64]{3,2,1,0:T(8,128)(2,1)S(1)}, bf16[32,2,16,64]{3,2,1,0:T(8,128)(2,1)S(1)}, u32[]{:S(2)}, u32[]{:S(2)}) collective-permute-start(bf16[32,2,16,64]{3,2,1,0:T(8,128)(2,1)S(1)} %get-tuple-element.136), channel_id=1, source_target_pairs={{0,31},{1,0},{2,1},{3,2},{4,3},{5,4},{6,5},{7,6},{8,7},{9,8},{10,9... | collective-permute-start | bytes 393224 | tf_op jit(solution)/shard_map/ppermute | solution.py:30
  522.6 3.0 copy-start.1
Sparse Core Ops, SparseCore 0:
  190.0 59.8 all-gather.1
where the time goes:
time: 543 us; the launch traced here: 533 us
  other arithmetic  266 us (49%)
  waiting for transfers between devices  98.1 us (18%)
  local copies, waits for them, and re-layouts  69.6 us (13%)
  matrix products  61.9 us (11%)
  starting transfers between devices  21.6 us (4%)
  between operations  14.9 us (3%)
    add x32, other arithmetic, add_source(): return running + product  129 us
    all_gather x1, waiting for transfers between devices, per_device(): lax.all_gather(top_pattern, 'box', axis=0, tiled=True)  54.1 us
    all_to_all x1, waiting for transfers between devices, per_device(): lax.all_to_all(rimmed, 'dir', split_axis=3, concat_axis=0, tiled=True)  36 us
    convert_element_type x32, other arithmetic, add_source(): lax.dynamic_index_in_dim(sources, source_row, 0, keepdims=False)  30.8 us
    convert_element_type x32, other arithmetic, add_source(): lax.dynamic_index_in_dim(coupling, source_row, 1, keepdims=False)  29.4 us
    dot_general x2, matrix products, lift_to_parents(): jnp.dot(member, turned.reshape(children, -1), precision=lax.Precision.HIG...  29.3 us
    another operation x1, local copies, waits for them, and re-layouts, turn(): jnp.stack([cosine * real_part - sine * imag_part, sine * real_part + cosi...  16.7 us
    dot_general x2, matrix products, interpolate(): jnp.einsum('bcrk,kn->bcrn', widened, matrices[0], preferred_element_type=...  16 us
  transfers between devices with their start and end apart: 6, of which 4 were waited for; matrix products, arithmetic and copies ran while one was open for 2% of the time, Pallas kernels for 0%

commit v1 on v0

v1 whole, which is shorter than its diff:
```python
import functools

import jax
import jax.numpy as jnp
from jax import lax
from jax.experimental import pallas as pl
from jax.experimental.pallas import tpu as pltpu
from jax.sharding import PartitionSpec as P

FS = 256
MS = 896
TS = 3328
HALO = 64
LANES = 128
KIDS = 4
TILE = 256
UNROLL = 4
BF = jnp.bfloat16
F32 = jnp.float32


def params(mib=60):
    return pltpu.CompilerParams(vmem_limit_bytes=mib * 1024 * 1024)


def low_lanes(shape):
    return lax.broadcasted_iota(jnp.int32, shape, len(shape) - 1) < HALO


def pack_kernel(x_ref, o_ref):
    sectors = o_ref.shape[0]
    low = low_lanes(x_ref.shape[1:2] + (LANES,))
    for s in range(sectors):
        o_ref[s, 0, :, :FS] = x_ref[0, :, s * FS : (s + 1) * FS]
        nxt = ((s + 1) % sectors) * FS
        prv = ((s - 1) % sectors) * FS + FS - LANES
        o_ref[s, 0, :, FS:] = jnp.where(
            low, x_ref[0, :, nxt : nxt + LANES], x_ref[0, :, prv : prv + LANES]
        )


def pack(fine, sectors):
    rows, columns, width = fine.shape
    return pl.pallas_call(
        pack_kernel,
        out_shape=jax.ShapeDtypeStruct((sectors, rows, columns, FS + LANES), BF),
        grid=(rows,),
        in_specs=[pl.BlockSpec((1, columns, width), lambda i: (i, 0, 0))],
        out_specs=pl.BlockSpec((sectors, 1, columns, FS + LANES), lambda i: (0, i, 0, 0)),
        compiler_params=params(),
        name="pack",
    )(fine)


def rotate_sum(values, first, position, cos_ref, sin_ref, row):
    real = imag = None
    for j in range(KIDS):
        p = position[first + j]
        c = cos_ref[pl.ds(p, 1), :]
        s = sin_ref[pl.ds(p, 1), :]
        u = values[(row + j) * 32 : (row + j) * 32 + 16]
        v = values[(row + j) * 32 + 16 : (row + j) * 32 + 32]
        re = c * u - s * v
        im = s * u + c * v
        real = re if real is None else real + re
        imag = im if imag is None else imag + im
    return real, imag


def fine_kernel(child, position, x_ref, w_ref, cos_ref, sin_ref, o_ref):
    per = 4

    def body(g, _):
        base = g * (per * KIDS)
        lhs = jnp.concatenate([x_ref[child[base + i]] for i in range(per * KIDS)], axis=0)
        values = jnp.dot(lhs, w_ref[...], preferred_element_type=F32)
        for m in range(per):
            real, imag = rotate_sum(
                values, base + m * KIDS, position, cos_ref, sin_ref, m * KIDS
            )
            o_ref[g * per + m, :16] = real.astype(BF)
            o_ref[g * per + m, 16:] = imag.astype(BF)
        return 0

    lax.fori_loop(0, o_ref.shape[0] // per, body, 0)


def lift_fine(child, position, x, w, cos, sin):
    boxes, rows, k = x.shape
    n = w.shape[1]
    return pl.pallas_call(
        fine_kernel,
        out_shape=jax.ShapeDtypeStruct((boxes // KIDS, rows, n), BF),
        grid_spec=pltpu.PrefetchScalarGridSpec(
            num_scalar_prefetch=2,
            grid=(1,),
            in_specs=[
                pl.BlockSpec((boxes, rows, k), lambda i, *_: (0, 0, 0)),
                pl.BlockSpec((k, n), lambda i, *_: (0, 0)),
                pl.BlockSpec(cos.shape, lambda i, *_: (0, 0)),
                pl.BlockSpec(sin.shape, lambda i, *_: (0, 0)),
            ],
            out_specs=pl.BlockSpec((boxes // KIDS, rows, n), lambda i, *_: (0, 0, 0)),
        ),
        compiler_params=params(),
        cost_estimate=pl.CostEstimate(
            flops=2 * boxes * rows * k * n, bytes_accessed=2 * boxes * rows * k, transcendentals=0
        ),
        name="lift_fine",
    )(child, position, x, w, cos, sin)


def mid_kernel(child, position, e_ref, c_ref, n_ref, p_ref, w_ref, cos_ref, sin_ref, o_ref, lhs):
    boxes, rows, _ = e_ref.shape
    edge = 2 * LANES
    inner = c_ref.shape[2]

    @pl.when(pl.program_id(0) == 0)
    def _():
        low = low_lanes((rows, LANES))

        def gather(i, _):
            m = child[i]
            at = pl.ds(pl.multiple_of(i * rows, rows), rows)
            lhs[at, :edge] = e_ref[m]
            lhs[at, edge : edge + inner] = c_ref[m]
            lhs[at, edge + inner :] = jnp.where(low, n_ref[m], p_ref[m])
            return 0

        lax.fori_loop(0, boxes, gather, 0)

    values = jnp.dot(lhs[...], w_ref[...], preferred_element_type=F32)
    for t in range(boxes // KIDS):
        real, imag = rotate_sum(values, t * KIDS, position, cos_ref, sin_ref, t * KIDS)
        o_ref[t, :16] = real.astype(BF)
        o_ref[t, 16:] = imag.astype(BF)


def lift_mid(child, position, edges, central, from_next, from_prev, w, cos, sin, first, tiles):
    boxes, rows, _ = edges.shape
    k = w.shape[0]
    whole = lambda a: pl.BlockSpec(a.shape, lambda i, *_: (0,) * a.ndim)
    return pl.pallas_call(
        mid_kernel,
        out_shape=jax.ShapeDtypeStruct((boxes // KIDS, rows, tiles * TILE), BF),
        grid_spec=pltpu.PrefetchScalarGridSpec(
            num_scalar_prefetch=2,
            grid=(tiles,),
            in_specs=[
                whole(edges),
                whole(central),
                whole(from_next),
                whole(from_prev),
                pl.BlockSpec((k, TILE), lambda i, *_: (0, i + first)),
                pl.BlockSpec((cos.shape[0], TILE), lambda i, *_: (0, i + first)),
                pl.BlockSpec((sin.shape[0], TILE), lambda i, *_: (0, i + first)),
            ],
            out_specs=pl.BlockSpec((boxes // KIDS, rows, TILE), lambda i, *_: (0, 0, i)),
            scratch_shapes=[pltpu.VMEM((boxes * rows, k), BF)],
        ),
        compiler_params=params(),
        cost_estimate=pl.CostEstimate(
            flops=2 * boxes * rows * k * tiles * TILE,
            bytes_accessed=2 * k * tiles * TILE,
            transcendentals=0,
        ),
        name="lift_mid",
    )(child, position, edges, central, from_next, from_prev, w, cos, sin)


def translate_kernel(
    starts, source, kind, group, child, position, *refs
):
    parts = refs[:4]
    op_ref, cos_ref, sin_ref, top_ref, spread_ref, held = refs[4:]
    group_size = parts[0].shape[0]
    for j in range(4):
        held[pl.ds((group[0] ^ j) * group_size, group_size)] = parts[j][...]

    def target(t, _):
        def pairs(i, carry):
            real, imag = carry
            for n in range(UNROLL):
                at = i * UNROLL + n
                u = source[at]
                k = kind[at]
                xr = held[u, :16].astype(F32)
                xi = held[u, 16:].astype(F32)
                tr = op_ref[k, 0:1, :]
                ti = op_ref[k, 1:2, :]
                real = real + tr * xr - ti * xi
                imag = imag + tr * xi + ti * xr
            return real, imag

        zero = jnp.zeros((16, held.shape[2]), F32)
        real, imag = lax.fori_loop(starts[t], starts[t + 1], pairs, (zero, zero))
        top_ref[t, 0] = real
        top_ref[t, 1] = imag
        real = real.astype(BF).astype(F32)
        imag = imag.astype(BF).astype(F32)
        for j in range(KIDS):
            m = child[t * KIDS + j]
            p = position[t * KIDS + j]
            c = cos_ref[pl.ds(p, 1), :]
            s = sin_ref[pl.ds(p, 1), :]
            spread_ref[m, :16] = (c * real + s * imag).astype(BF)
            spread_ref[m, 16:] = (c * imag - s * real).astype(BF)
        return 0

    lax.fori_loop(0, group_size, target, 0)


def translate(starts, source, kind, group, child, position, parts, operators, cos, sin):
    size, rows, width = parts[0].shape
    mids = size * KIDS
    tiles = width // TILE
    part = pl.BlockSpec((size, rows, TILE), lambda i, *_: (0, 0, i))
    return pl.pallas_call(
        translate_kernel,
        out_shape=(
            jax.ShapeDtypeStruct((size, 2, rows // 2, width), F32),
            jax.ShapeDtypeStruct((mids, rows, width), BF),
        ),
        grid_spec=pltpu.PrefetchScalarGridSpec(
            num_scalar_prefetch=6,
            grid=(tiles,),
            in_specs=[part] * 4
            + [
                pl.BlockSpec(operators.shape[:2] + (TILE,), lambda i, *_: (0, 0, i)),
                pl.BlockSpec((cos.shape[0], TILE), lambda i, *_: (0, i)),
                pl.BlockSpec((sin.shape[0], TILE), lambda i, *_: (0, i)),
            ],
            out_specs=(
                pl.BlockSpec((size, 2, rows // 2, TILE), lambda i, *_: (0, 0, 0, i)),
                pl.BlockSpec((mids, rows, TILE), lambda i, *_: (0, 0, i)),
            ),
            scratch_shapes=[pltpu.VMEM((4 * size, rows, TILE), BF)],
        ),
        compiler_params=params(),
        name="translate",
    )(starts, source, kind, group, child, position, *parts, operators, cos, sin)


def edge_kernel(x_ref, p_ref, n_ref, o_ref):
    low = low_lanes(p_ref.shape)
    first = pl.program_id(0) == 0
    take = jnp.where(first, p_ref[...].astype(F32), n_ref[...].astype(F32))
    o_ref[...] = x_ref[...] + jnp.where(low == first, take, 0.0)


def add_edges(central, from_prev, from_next):
    boxes, rows, width = central.shape
    last = width // LANES - 1
    tile = pl.BlockSpec((boxes, rows, LANES), lambda i: (0, 0, i * last))
    halo = pl.BlockSpec((boxes, rows, LANES), lambda i: (0, 0, 0))
    return pl.pallas_call(
        edge_kernel,
        out_shape=jax.ShapeDtypeStruct(central.shape, F32),
        grid=(2,),
        in_specs=[tile, halo, halo],
        out_specs=tile,
        input_output_aliases={0: 0},
        compiler_params=params(),
        name="add_edges",
    )(central, from_prev, from_next)


def children_of(parents, positions, count):
    n = parents.shape[0]
    index = jnp.arange(n, dtype=jnp.int32)
    before = (parents[None, :] < parents[:, None]) | (
        (parents[None, :] == parents[:, None]) & (index[None, :] < index[:, None])
    )
    rank = jnp.sum(before.astype(jnp.int32), axis=1)
    match = (rank[None, :] == index[:, None]).astype(jnp.int32)
    return (
        jnp.sum(match * index[None, :], axis=1),
        jnp.sum(match * positions[None, :], axis=1),
    )


def pair_lists(target, source, kind, base, count, kinds):
    pairs = target.shape[0]
    index = jnp.arange(pairs, dtype=jnp.int32)
    local = target - base
    boxes = jnp.arange(count, dtype=jnp.int32)
    mine = local[None, :] == boxes[:, None]
    padded = (jnp.sum(mine.astype(jnp.int32), axis=1) + UNROLL - 1) // UNROLL
    starts = jnp.sum(
        jnp.where(
            boxes[None, :] < jnp.arange(count + 1, dtype=jnp.int32)[:, None], padded[None, :], 0
        ),
        axis=1,
    )
    earlier = (local[None, :] == local[:, None]) & (index[None, :] < index[:, None])
    within = jnp.sum(earlier.astype(jnp.int32), axis=1)
    begin = jnp.sum(jnp.where(mine, starts[:count, None] * UNROLL, 0), axis=0)
    slot = jnp.where(jnp.any(mine, axis=0), begin + within, -1)
    slots = pairs + count * (UNROLL - 1)
    match = (slot[None, :] == jnp.arange(slots, dtype=jnp.int32)[:, None]).astype(jnp.int32)
    return (
        starts,
        jnp.sum(match * source[None, :], axis=1),
        kinds + jnp.sum(match * (kind - kinds)[None, :], axis=1),
    )


def per_device(
    fine_pattern,
    fine_interp,
    mid_interp,
    fine_angle,
    top_angle,
    translator,
    fine_position,
    mid_position,
    fine_parent,
    mid_parent,
    pair_target,
    pair_source,
    pair_kind,
):
    box = lax.axis_index("box")
    dirs = lax.axis_size("dir")
    fine_local, _, columns, width = fine_pattern.shape
    rows = 2 * columns
    fine_group = fine_local * dirs
    mid_group = fine_group // KIDS
    top_group = mid_group // KIDS
    kinds = translator.shape[0]
    up = [(i, (i + 1) % dirs) for i in range(dirs)]
    down = [((i + 1) % dirs, i) for i in range(dirs)]

    packed = pack(fine_pattern.reshape(fine_local * 2, columns, width), dirs)
    arrived = lax.all_to_all(packed, "dir", split_axis=0, concat_axis=0, tiled=True)
    arrived = arrived.reshape(fine_group, rows, FS + LANES)

    cut = lambda a, n: lax.dynamic_slice_in_dim(a, box * n, n)
    fine_child, fine_pos = children_of(
        cut(fine_parent, fine_group), cut(fine_position, fine_group), mid_group
    )
    mid_child, mid_pos = children_of(
        cut(mid_parent, mid_group), cut(mid_position, mid_group), top_group
    )
    starts, source, kind = pair_lists(
        pair_target, pair_source, pair_kind, box * top_group, top_group, kinds
    )
    fine_cos, fine_sin = jnp.cos(fine_angle), jnp.sin(fine_angle)
    top_cos, top_sin = jnp.cos(top_angle), jnp.sin(top_angle)
    operators = jnp.concatenate(
        [translator.astype(F32), jnp.zeros((8,) + translator.shape[1:], F32)], axis=0
    )
    wf = fine_interp[0]
    wf = jnp.concatenate([wf[HALO : HALO + FS], wf[HALO + FS :], wf[:HALO]], axis=0)
    wm = mid_interp[0]
    last = HALO + MS - LANES
    wm_halo = jnp.concatenate([wm[HALO + MS :], wm[:HALO]], axis=0)
    wm_central = wm[HALO : HALO + MS]
    wm_up = jnp.concatenate(
        [wm[HALO : HALO + LANES], wm[last : HALO + MS], wm[HALO + LANES : last], wm_halo], axis=0
    )
    ends = lambda a: jnp.concatenate([a[:, :LANES], a[:, MS - LANES :]], axis=1)
    inside = lambda a: a[:, LANES : MS - LANES]

    edges = lift_fine(fine_child, fine_pos, arrived, ends(wf), ends(fine_cos), ends(fine_sin))
    from_next = lax.ppermute(edges[:, :, :LANES], "dir", down)
    from_prev = lax.ppermute(edges[:, :, LANES:], "dir", up)
    central = lift_fine(
        fine_child, fine_pos, arrived, inside(wf), inside(fine_cos), inside(fine_sin)
    )
    top = lift_mid(
        mid_child, mid_pos, edges, central, from_next, from_prev, wm_up, top_cos, top_sin, 0,
        TS // TILE,
    )
    core = [(i, i ^ 1) for i in range(4)]
    far = [(i, i ^ 2) for i in range(4)]
    top_core = lax.ppermute(top, "box", core)
    top_far = lax.ppermute(top, "box", far)
    top_both = lax.ppermute(top_far, "box", core)
    top_incoming, spread = translate(
        starts, source, kind, box[None], mid_child, mid_pos,
        (top, top_core, top_far, top_both), operators, top_cos, top_sin,
    )
    halo = jnp.einsum("bxn,kn->bxk", spread, wm_halo, preferred_element_type=F32).astype(BF)
    below = lax.ppermute(halo, "dir", up)
    above = lax.ppermute(halo, "dir", down)
    middle = jnp.einsum("bxn,kn->bxk", spread, wm_central, preferred_element_type=F32)
    mid_incoming = add_edges(middle, below, above)
    return top_incoming, mid_incoming.reshape(mid_group, 2, columns, MS)


def solution(mesh):
    placed = (
        P(("box", "dir"), None, None, None),
        P("dir", None, None),
        P("dir", None, None),
        P(None, "dir"),
        P(None, "dir"),
        P(None, None, "dir"),
        P(),
        P(),
        P(),
        P(),
        P(),
        P(),
        P(),
    )
    return jax.shard_map(
        per_device,
        mesh=mesh,
        in_specs=placed,
        out_specs=(P("box", None, None, "dir"), P("box", None, None, "dir")),
        check_vma=False,
    )
```

time: 543 us -> 191 us (0.35); the launches traced: 533 us -> 189 us
  other arithmetic: 266 us -> 8.36 us
  Pallas kernels: 0 us -> 55.4 us
  matrix products: 61.9 us -> 15.6 us
  waiting for transfers between devices: 98.1 us -> 54 us
  local copies, waits for them, and re-layouts: 69.6 us -> 26.3 us
  between operations: 14.9 us -> 0.81 us
  starting transfers between devices: 21.6 us -> 28.7 us
    add x33 -> x1, other arithmetic: 132 us -> 0.6 us  [pair_lists(): kinds + jnp.sum(match * (kind - kinds)[None, :], axis=1)]
    convert_element_type x67 -> x0, other arithmetic: 62.3 us -> none  [the longest x32 30.8 us: add_source(): lax.dynamic_index_in_dim(sources, source_row, 0, keepdims=False)]
    pallas_call x0 -> x6, Pallas kernels: none -> 55.4 us  [the longest x1 17.6 us: translate(): pl.pallas_call(translate_kernel, out_shape=(jax.ShapeDtypeStruct((size, 2...]
    all_gather x1 -> x0, waiting for transfers between devices: 54.1 us -> none  [per_device(): lax.all_gather(top_pattern, 'box', axis=0, tiled=True)]
    dot_general x8 -> x2, matrix products: 61.9 us -> 15.6 us  [the longest x1 10.6 us: per_device(): jnp.einsum('bxn,kn->bxk', spread, wm_central, preferred_element_type=F32)]
    ppermute x4 -> x7, waiting for transfers between devices: 7.91 us -> 35.4 us  [the longest x1 33.1 us: per_device(): top_far = lax.ppermute(top, 'box', far)]
    another operation x3 -> x0, other arithmetic: 27.3 us -> none
    sub x34 -> x1, other arithmetic: 26.8 us -> 0.01 us  [pair_lists(): local = target - base]
  transfers between devices with their start and end apart: 6 -> 8, of which waited for: 4 -> 3; matrix products, arithmetic and copies ran while one was open for 2% -> 20% of each run, Pallas kernels for 0% -> 4%
where the time goes in v1:
time: 191 us; the launch traced here: 189 us
  Pallas kernels  55.4 us (29%)
  waiting for transfers between devices  54 us (28%)
  starting transfers between devices  28.7 us (15%)
  local copies, waits for them, and re-layouts  26.3 us (14%)
  matrix products  15.6 us (8%)
  other arithmetic  8.36 us (4%)
    ppermute x1, waiting for transfers between devices, per_device(): top_far = lax.ppermute(top, 'box', far)  33.1 us
    all_to_all x1, waiting for transfers between devices, per_device(): lax.all_to_all(packed, 'dir', split_axis=0, concat_axis=0, tiled=True)  18.6 us
    pallas_call x1, Pallas kernels, translate(): pl.pallas_call(translate_kernel, out_shape=(jax.ShapeDtypeStruct((size, 2...  17.6 us
    unnamed x42, local copies, waits for them, and re-layouts  16.2 us
    pallas_call x1, Pallas kernels, lift_mid(): pl.pallas_call(mid_kernel, out_shape=jax.ShapeDtypeStruct((boxes // KIDS,...  15.5 us
    pallas_call x2, Pallas kernels, lift_fine(): pl.pallas_call(fine_kernel, out_shape=jax.ShapeDtypeStruct((boxes // KIDS...  14 us
    dot_general x1, matrix products, per_device(): jnp.einsum('bxn,kn->bxk', spread, wm_central, preferred_element_type=F32)  10.6 us
    all_to_all x1, starting transfers between devices, per_device(): lax.all_to_all(packed, 'dir', split_axis=0, concat_axis=0, tiled=True)  9.34 us
  transfers between devices with their start and end apart: 8, of which 3 were waited for; matrix products, arithmetic and copies ran while one was open for 20% of the time, Pallas kernels for 4%

profile of v1, /device:TPU:1, one launch (start us, length us, event | category | flops | bytes accessed | tf_op | source)
XLA Modules:
  0.0 189.2 jit_solution(3879027230970019610)
XLA Ops:
  0.7 5.9 %pack.1 = bf16[32,8,16,384]{3,2,1,0:T(8,128)(2,1)} custom-call(bf16[8,16,8192]{2,1,0:T(8,128)(2,1)} %bitcast.38), custom_call_target="tpu_custom_call" | custom-call | tf_op jit(solution)/shard_map/pack/pallas_call | solution.py:44
  6.6 9.3 %all-to-all-start = ((bf16[32,8,16,384]{3,2,1,0:T(8,128)(2,1)}), bf16[32,8,16,384]{3,2,1,0:T(8,128)(2,1)S(1)}, u32[]{:S(2)}, u32[]{:S(2)}) async-start(bf16[32,8,16,384]{3,2,1,0:T(8,128)(2,1)} %pack.1), calls=%async_computation | async-start | bytes 6291456 | tf_op jit(solution)/shard_map/all_to_all | solution.py:335
  15.9 1.0 slice_bitcast_fusion.4
  16.9 1.1 slice_bitcast_fusion
  18.0 0.7 fusion.14.w_ref
  18.7 0.8 pad_maximum_fusion.w_ref
  19.5 0.8 dynamic_slice.14
  20.4 0.8 dynamic_slice.15
  21.4 0.2 convert_reduce_fusion.2
  21.6 1.1 fusion.24
  22.7 2.1 %bitcast_dynamic-update-slice_fusion.2 = bf16[1024,3328]{1,0:T(8,128)(2,1)} fusion(bf16[1,1024,3328]{2,1,0:T(8,128)(2,1)} %param.15), kind=kLoop, calls=%fused_computation.10 | loop fusion | bytes 1703936
  24.8 2.1 %bitcast_dynamic-update-slice_fusion.1 = bf16[1024,3328]{1,0:T(8,128)(2,1)} fusion(bf16[1024,3328]{1,0:T(8,128)(2,1)} %bitcast_dynamic-update-slice_fusion.2, bf16[1,1024,3328]{2,1,0:T(8,128)(2,1)} %param.15), kind=kLoop, calls=%fused_computation.9 | loop fusion | bytes 1703936
  27.0 0.7 select_reduce_fusion.2
  27.7 0.6 pad_maximum_fusion.2.cos_ref
  28.2 0.6 pad_maximum_fusion.3.sin_ref
  28.8 0.6 slice.124.cos_ref
  29.4 0.6 slice.125.sin_ref
  30.1 4.5 %bitcast_dynamic-update-slice_fusion = bf16[1024,3328]{1,0:T(8,128)(2,1)} fusion(bf16[1024,3328]{1,0:T(8,128)(2,1)} %bitcast_dynamic-update-slice_fusion.1, bf16[1,1024,3328]{2,1,0:T(8,128)(2,1)} %param.15), kind=kLoop, calls=%fused_computation.3 | loop fusion | bytes 8519680
  34.7 1.8 constant_dynamic-update-slice_fusion.1
  36.4 1.8 constant_dynamic-update-slice_fusion.w_ref
  38.2 18.6 %all-to-all-done = bf16[32,8,16,384]{3,2,1,0:T(8,128)(2,1)S(1)} async-done(((bf16[32,8,16,384]{3,2,1,0:T(8,128)(2,1)}), bf16[32,8,16,384]{3,2,1,0:T(8,128)(2,1)S(1)}, u32[]{:S(2)}, u32[]{:S(2)}) %all-to-all-start) | async-done | bytes 3145760 | tf_op jit(solution)/shard_map/all_to_all | solution.py:335
  56.9 1.7 copy-done
  58.5 5.9 %lift_fine.2.e_ref = bf16[32,32,256]{2,1,0:T(8,128)(2,1)} custom-call(s32[128]{0:T(128)} %get-tuple-element.9.child, s32[128]{0:T(128)} %get-tuple-element.8.position, bf16[128,32,384]{2,1,0:T(8,128)(2,1)} %bitcast.33, bf16[384,256]{1,0:T(8,128)(2,1)} %fusion.14.w_ref, f32[8,256]{1,0:T(8,128)} %pad_maximum_fusion.2.cos_ref, f32[8,256]{1,0:T(8,128)} %pad_maximum_fusion.3.sin_ref), custom_call_target="tpu_custom_call" | custom-call | flops 805306368 | bytes 3145728 | tf_op jit(solution)/shard_map/lift_fine/pallas_call | solution.py:91
  64.4 1.1 fusion.23
  65.5 5.6 %collective-permute-start = (bf16[32,32,128]{2,1,0:T(8,128)(2,1)S(1)}, bf16[32,32,128]{2,1,0:T(8,128)(2,1)S(1)}, u32[]{:S(2)}, u32[]{:S(2)}) collective-permute-start(bf16[32,32,128]{2,1,0:T(8,128)(2,1)S(1)} %get-tuple-element.17), channel_id=1, source_target_pairs={{1,0},{2,1},{3,2},{4,3},{5,4},{6,5},{7,6},{8,7},{9,8},{10,9},{11,1... | collective-permute-start | bytes 786440 | tf_op jit(solution)/shard_map/ppermute | solution.py:366
  71.1 0.7 select_reduce_fusion.4
  71.8 8.1 %lift_fine.3.c_ref = bf16[32,32,640]{2,1,0:T(8,128)(2,1)} custom-call(s32[128]{0:T(128)} %get-tuple-element.9.child, s32[128]{0:T(128)} %get-tuple-element.8.position, bf16[128,32,384]{2,1,0:T(8,128)(2,1)} %bitcast.34, bf16[384,640]{1,0:T(8,128)(2,1)} %pad_maximum_fusion.w_ref, f32[8,640]{1,0:T(8,128)} %slice.124.cos_ref, f32[8,640]{1,0:T(8,128)} %slice.125.sin_ref), custom_call_target="tpu_custom_call" | custom-call | flops 2013265920 | bytes 3145728 | tf_op jit(solution)/shard_map/lift_fine/pallas_call | solution.py:91
  79.9 2.3 %collective-permute-done.1.p_ref = bf16[32,32,128]{2,1,0:T(8,128)(2,1)S(1)} collective-permute-done((bf16[32,32,128]{2,1,0:T(8,128)(2,1)S(1)}, bf16[32,32,128]{2,1,0:T(8,128)(2,1)S(1)}, u32[]{:S(2)}, u32[]{:S(2)}) %collective-permute-start.1) | collective-permute-done | bytes 262176 | tf_op jit(solution)/shard_map/ppermute | solution.py:367
  82.2 0.7 copy-done.14
  82.9 15.5 %lift_mid.1.refs_0_ = bf16[8,32,3328]{2,1,0:T(8,128)(2,1)} custom-call(s32[32]{0:T(128)} %get-tuple-element.11.child, s32[32]{0:T(128)} %get-tuple-element.10.position, bf16[32,32,256]{2,1,0:T(8,128)(2,1)} %lift_fine.2.e_ref, bf16[32,32,640]{2,1,0:T(8,128)(2,1)} %lift_fine.3.c_ref, bf16[32,32,128]{2,1,0:T(8,128)(2,1)} %copy-done.13, ...), custom_call_target="tpu_custom_call" | custom-call | flops 6979321856 | bytes 6815744 | tf_op jit(solution)/shard_map/lift_mid/pallas_call | solution.py:143
  98.4 3.3 %collective-permute-start.3 = (bf16[8,32,3328]{2,1,0:T(8,128)(2,1)}, bf16[8,32,3328]{2,1,0:T(8,128)(2,1)S(1)}, u32[]{:S(2)}, u32[]{:S(2)}) collective-permute-start(bf16[8,32,3328]{2,1,0:T(8,128)(2,1)} %lift_mid.1.refs_0_), channel_id=1, source_target_pairs={{0,64},{32,96},{64,0},{96,32},{1,65},{33,97},{65,1},{97,33},{2,66}... | collective-permute-start | bytes 5111816 | tf_op jit(solution)/shard_map/ppermute | solution.py:378
  102.1 0.2 convert_reduce_fusion
  102.3 2.2 %collective-permute-start.2 = (bf16[8,32,3328]{2,1,0:T(8,128)(2,1)}, bf16[8,32,3328]{2,1,0:T(8,128)(2,1)S(1)}, u32[]{:S(2)}, u32[]{:S(2)}) collective-permute-start(bf16[8,32,3328]{2,1,0:T(8,128)(2,1)} %lift_mid.1.refs_0_), channel_id=1, source_target_pairs={{0,32},{32,0},{64,96},{96,64},{1,33},{33,1},{65,97},{97,65},{2,34}... | collective-permute-start | bytes 5111816 | tf_op jit(solution)/shard_map/ppermute | solution.py:377
  104.5 33.1 %collective-permute-done.3.refs_2_ = bf16[8,32,3328]{2,1,0:T(8,128)(2,1)S(1)} collective-permute-done((bf16[8,32,3328]{2,1,0:T(8,128)(2,1)}, bf16[8,32,3328]{2,1,0:T(8,128)(2,1)S(1)}, u32[]{:S(2)}, u32[]{:S(2)}) %collective-permute-start.3) | collective-permute-done | bytes 1703968 | tf_op jit(solution)/shard_map/ppermute | solution.py:378
  137.6 2.5 %collective-permute-start.4 = (bf16[8,32,3328]{2,1,0:T(8,128)(2,1)S(1)}, bf16[8,32,3328]{2,1,0:T(8,128)(2,1)S(1)}, u32[]{:S(2)}, u32[]{:S(2)}) collective-permute-start(bf16[8,32,3328]{2,1,0:T(8,128)(2,1)S(1)} %collective-permute-done.3.refs_2_), channel_id=1, source_target_pairs={{0,32},{32,0},{64,96},{96,64},{1,33},{33,1},{65,97},{97,65},{2,34}... | collective-permute-start | bytes 5111816 | tf_op jit(solution)/shard_map/ppermute | solution.py:379
  140.1 0.8 select_reduce_fusion
  140.9 0.6 broadcast_add_fusion.kind
  141.5 2.0 %pad_convert_fusion.refs_4_ = f32[72,2,3328]{2,1,0:T(2,128)} fusion(bf16[64,2,3328]{2,1,0:T(2,128)(2,1)S(1)} %copy-done.4), kind=kLoop, calls=%fused_computation.5 | loop fusion | flops 479232 | bytes 2768896 | tf_op jit(solution)/shard_map/concatenate | solution.py:350
  143.5 1.2 slice_bitcast_fusion.2
  144.7 1.2 copy-done.2
  146.0 0.5 copy-done.3
  146.5 17.6 %translate.1 = (f32[8,2,16,3328]{3,2,1,0:T(8,128)}, bf16[32,32,3328]{2,1,0:T(8,128)(2,1)}) custom-call(s32[9]{0:T(128)} %copy-done.12, s32[280]{0:T(512)} %get-tuple-element.7.source, s32[280]{0:T(512)} %broadcast_add_fusion.kind, s32[1]{0:T(128)} %bitcast.group, s32[32]{0:T(128)} %get-tuple-element.11.child, s32[32]{0:T(128)} %get-tuple-element.10.position, ...), custom_call_target="tpu_custom_call" | custom-call | tf_op jit(solution)/shard_map/translate/pallas_call | solution.py:218
  164.1 5.0 %convolution_convert_fusion = bf16[32,32,128]{2,1,0:T(8,128)(2,1)S(1)} fusion(bf16[32,32,3328]{2,1,0:T(8,128)(2,1)} %get-tuple-element.5, bf16[64,3328]{1,0:T(8,128)(2,1)S(1)} %get-tuple-element.13, bf16[64,3328]{1,0:T(8,128)(2,1)S(1)} %get-tuple-element.12), kind=kOutput, calls=%fused_computation.4 | convolution fusion | flops 874250240 | bytes 7929856 | tf_op jit(solution)/shard_map/bxn,kn->bxk/dot_general | solution.py:384
  169.2 5.7 %collective-permute-start.6 = (bf16[32,32,128]{2,1,0:T(8,128)(2,1)S(1)}, bf16[32,32,128]{2,1,0:T(8,128)(2,1)S(1)}, u32[]{:S(2)}, u32[]{:S(2)}) collective-permute-start(bf16[32,32,128]{2,1,0:T(8,128)(2,1)S(1)} %convolution_convert_fusion), channel_id=1, source_target_pairs={{1,0},{2,1},{3,2},{4,3},{5,4},{6,5},{7,6},{8,7},{9,8},{10,9},{11,1... | collective-permute-start | bytes 786440 | tf_op jit(solution)/shard_map/ppermute | solution.py:386
  174.9 10.6 %fusion.x_ref = f32[32,32,896]{2,1,0:T(8,128)} fusion(bf16[32,32,3328]{2,1,0:T(8,128)(2,1)} %get-tuple-element.5, bf16[1,1024,3328]{2,1,0:T(8,128)(2,1)S(1)} %bitcast.36), kind=kOutput, calls=%fused_computation | convolution fusion | flops 6106906624 | bytes 16449536 | tf_op jit(solution)/shard_map/bxn,kn->bxk/dot_general | solution.py:387
  185.5 0.7 copy-done.5
  186.2 0.7 copy-done.6
  186.9 2.2 %add_edges.1 = f32[32,32,896]{2,1,0:T(8,128)} custom-call(f32[32,32,896]{2,1,0:T(8,128)} %fusion.x_ref, bf16[32,32,128]{2,1,0:T(8,128)(2,1)} %copy-done.5, bf16[32,32,128]{2,1,0:T(8,128)(2,1)} %copy-done.6), custom_call_target="tpu_custom_call", output_to_operand_aliasing={{}: (0, {})} | custom-call | tf_op jit(solution)/shard_map/add_edges/pallas_call | solution.py:256
  (53 shorter events, 0.9 us)
Async XLA Ops:
  0.6 20.6 %copy-start.8 = (f32[8,896]{1,0:T(8,128)S(1)}, f32[8,896]{1,0:T(8,128)}, u32[]{:S(2)}) copy-start(f32[8,896]{1,0:T(8,128)} %param.16) | copy-start | bytes 86020
  0.6 20.7 %copy-start.15 = (s32[128]{0:T(128)S(1)}, s32[128]{0:T(128)}, u32[]{:S(2)}) copy-start(s32[128]{0:T(128)} %param.22) | copy-start | bytes 1540
  0.7 21.0 %copy-start.7 = (f32[8,3328]{1,0:T(8,128)S(1)}, f32[8,3328]{1,0:T(8,128)}, u32[]{:S(2)}) copy-start(f32[8,3328]{1,0:T(8,128)} %param.17) | copy-start | bytes 319492
  6.6 23.5 %copy-start.16 = (s32[128]{0:T(128)S(1)}, s32[128]{0:T(128)}, u32[]{:S(2)}) copy-start(s32[128]{0:T(128)} %param.20) | copy-start | bytes 1540
  6.6 50.3 %all-to-all-start = ((bf16[32,8,16,384]{3,2,1,0:T(8,128)(2,1)}), bf16[32,8,16,384]{3,2,1,0:T(8,128)(2,1)S(1)}, u32[]{:S(2)}, u32[]{:S(2)}) async-start(bf16[32,8,16,384]{3,2,1,0:T(8,128)(2,1)} %pack.1), calls=%async_computation | async-start | bytes 6291456 | tf_op jit(solution)/shard_map/all_to_all | solution.py:335
  56.9 1.7 copy-start
  65.5 14.4 %collective-permute-start = (bf16[32,32,128]{2,1,0:T(8,128)(2,1)S(1)}, bf16[32,32,128]{2,1,0:T(8,128)(2,1)S(1)}, u32[]{:S(2)}, u32[]{:S(2)}) collective-permute-start(bf16[32,32,128]{2,1,0:T(8,128)(2,1)S(1)} %get-tuple-element.17), channel_id=1, source_target_pairs={{1,0},{2,1},{3,2},{4,3},{5,4},{6,5},{7,6},{8,7},{9,8},{10,9},{11,1... | collective-permute-start | bytes 786440 | tf_op jit(solution)/shard_map/ppermute | solution.py:366
  71.1 11.1 %collective-permute-start.1 = (bf16[32,32,128]{2,1,0:T(8,128)(2,1)S(1)}, bf16[32,32,128]{2,1,0:T(8,128)(2,1)S(1)}, u32[]{:S(2)}, u32[]{:S(2)}) collective-permute-start(bf16[32,32,128]{2,1,0:T(8,128)(2,1)S(1)} %get-tuple-element.16), channel_id=1, source_target_pairs={{0,1},{1,2},{2,3},{3,4},{4,5},{5,6},{6,7},{7,8},{8,9},{9,10},{10,1... | collective-permute-start | bytes 786440 | tf_op jit(solution)/shard_map/ppermute | solution.py:367
  79.9 2.3 %copy-start.13 = (bf16[32,32,128]{2,1,0:T(8,128)(2,1)}, bf16[32,32,128]{2,1,0:T(8,128)(2,1)S(1)}, u32[]{:S(2)}) copy-start(bf16[32,32,128]{2,1,0:T(8,128)(2,1)S(1)} %collective-permute-done.n_ref) | copy-start | bytes 786436
  82.2 0.7 copy-start.14
  82.9 18.8 %copy-start.10 = (s32[256]{0:T(256)S(1)}, s32[256]{0:T(256)}, u32[]{:S(2)}) copy-start(s32[256]{0:T(256)} %param.23) | copy-start | bytes 3076
  82.9 19.4 %copy-start.11 = (s32[256]{0:T(256)S(1)}, s32[256]{0:T(256)}, u32[]{:S(2)}) copy-start(s32[256]{0:T(256)} %param.25) | copy-start | bytes 3076
  82.9 57.2 %copy-start.9 = (s32[256]{0:T(256)S(1)}, s32[256]{0:T(256)}, u32[]{:S(2)}) copy-start(s32[256]{0:T(256)} %param.24) | copy-start | bytes 3076
  82.9 58.6 %copy-start.4 = (bf16[64,2,3328]{2,1,0:T(2,128)(2,1)S(1)}, bf16[64,2,3328]{2,1,0:T(2,128)(2,1)}, u32[]{:S(2)}) copy-start(bf16[64,2,3328]{2,1,0:T(2,128)(2,1)} %param.18) | copy-start | bytes 2555908
  98.4 39.2 %collective-permute-start.3 = (bf16[8,32,3328]{2,1,0:T(8,128)(2,1)}, bf16[8,32,3328]{2,1,0:T(8,128)(2,1)S(1)}, u32[]{:S(2)}, u32[]{:S(2)}) collective-permute-start(bf16[8,32,3328]{2,1,0:T(8,128)(2,1)} %lift_mid.1.refs_0_), channel_id=1, source_target_pairs={{0,64},{32,96},{64,0},{96,32},{1,65},{33,97},{65,1},{97,33},{2,66}... | collective-permute-start | bytes 5111816 | tf_op jit(solution)/shard_map/ppermute | solution.py:378
  102.0 44.5 %copy-start.12 = (s32[9]{0:T(128)}, s32[9]{0:T(128)S(1)}, u32[]{:S(2)}) copy-start(s32[9]{0:T(128)S(1)} %select_reduce_fusion.7.starts) | copy-start | bytes 112
  102.3 42.4 %collective-permute-start.2 = (bf16[8,32,3328]{2,1,0:T(8,128)(2,1)}, bf16[8,32,3328]{2,1,0:T(8,128)(2,1)S(1)}, u32[]{:S(2)}, u32[]{:S(2)}) collective-permute-start(bf16[8,32,3328]{2,1,0:T(8,128)(2,1)} %lift_mid.1.refs_0_), channel_id=1, source_target_pairs={{0,32},{32,0},{64,96},{96,64},{1,33},{33,1},{65,97},{97,65},{2,34}... | collective-permute-start | bytes 5111816 | tf_op jit(solution)/shard_map/ppermute | solution.py:377
  137.6 7.1 %copy-start.1 = (bf16[8,32,3328]{2,1,0:T(8,128)(2,1)}, bf16[8,32,3328]{2,1,0:T(8,128)(2,1)S(1)}, u32[]{:S(2)}) copy-start(bf16[8,32,3328]{2,1,0:T(8,128)(2,1)S(1)} %collective-permute-done.3.refs_2_) | copy-start | bytes 5111812
  137.6 7.1 %collective-permute-start.4 = (bf16[8,32,3328]{2,1,0:T(8,128)(2,1)S(1)}, bf16[8,32,3328]{2,1,0:T(8,128)(2,1)S(1)}, u32[]{:S(2)}, u32[]{:S(2)}) collective-permute-start(bf16[8,32,3328]{2,1,0:T(8,128)(2,1)S(1)} %collective-permute-done.3.refs_2_), channel_id=1, source_target_pairs={{0,32},{32,0},{64,96},{96,64},{1,33},{33,1},{65,97},{97,65},{2,34}... | collective-permute-start | bytes 5111816 | tf_op jit(solution)/shard_map/ppermute | solution.py:379
  144.7 1.3 copy-start.2
  144.7 1.8 copy-start.3
  146.5 28.4 %slice-start = ((s8[6815744]{0:T(1024)(128)(4,1)}), s8[2621440]{0:T(1024)(128)(4,1)S(1)}, s32[]{:S(2)}) async-start(s8[6815744]{0:T(1024)(128)(4,1)} %bitcast.35), calls=%async_computation.1 | async-start | bytes 5242880
  164.1 10.8 %slice-start.1 = ((s8[6815744]{0:T(1024)(128)(4,1)}), s8[4194304]{0:T(1024)(128)(4,1)S(1)}, s32[]{:S(2)}) async-start(s8[6815744]{0:T(1024)(128)(4,1)} %bitcast.35), calls=%async_computation.2 | async-start | bytes 8388608
  169.1 16.4 %collective-permute-start.5 = (bf16[32,32,128]{2,1,0:T(8,128)(2,1)S(1)}, bf16[32,32,128]{2,1,0:T(8,128)(2,1)S(1)}, u32[]{:S(2)}, u32[]{:S(2)}) collective-permute-start(bf16[32,32,128]{2,1,0:T(8,128)(2,1)S(1)} %convolution_convert_fusion), channel_id=1, source_target_pairs={{0,1},{1,2},{2,3},{3,4},{4,5},{5,6},{6,7},{7,8},{8,9},{9,10},{10,1... | collective-permute-start | bytes 786440 | tf_op jit(solution)/shard_map/ppermute | solution.py:385
  169.2 16.3 %collective-permute-start.6 = (bf16[32,32,128]{2,1,0:T(8,128)(2,1)S(1)}, bf16[32,32,128]{2,1,0:T(8,128)(2,1)S(1)}, u32[]{:S(2)}, u32[]{:S(2)}) collective-permute-start(bf16[32,32,128]{2,1,0:T(8,128)(2,1)S(1)} %convolution_convert_fusion), channel_id=1, source_target_pairs={{1,0},{2,1},{3,2},{4,3},{5,4},{6,5},{7,6},{8,7},{9,8},{10,9},{11,1... | collective-permute-start | bytes 786440 | tf_op jit(solution)/shard_map/ppermute | solution.py:386
  185.5 0.7 copy-start.5
  186.2 0.7 copy-start.6

commit v2 on v1

v2 whole, which is shorter than its diff:
```python
import jax
import jax.numpy as jnp
from jax import lax
from jax.experimental import pallas as pl
from jax.experimental.pallas import tpu as pltpu
from jax.sharding import PartitionSpec as P


FS = 256
MS = 896
HALO = 64
LANES = 128
KIDS = 4
TILE = 256
UNROLL = 4
CHUNKS = (2, 4, 4, 3)
BF = jnp.bfloat16
F32 = jnp.float32


def params(mib):
    return pltpu.CompilerParams(vmem_limit_bytes=mib * 1024 * 1024)


def low_lanes(shape):
    return lax.broadcasted_iota(jnp.int32, shape, len(shape) - 1) < HALO


def pack_kernel(x_hbm, o_hbm, x_ref, o_ref, in_sem, out_sem):
    rows, columns, _ = x_ref.shape
    sectors = o_ref.shape[1]
    low = low_lanes((columns, LANES))
    loads = [pltpu.make_async_copy(x_hbm.at[i], x_ref.at[i], in_sem.at[i]) for i in range(rows)]
    stores = [
        pltpu.make_async_copy(o_ref.at[i], o_hbm.at[:, i], out_sem.at[i]) for i in range(rows)
    ]
    for load in loads:
        load.start()
    for i in range(rows):
        loads[i].wait()
        for s in range(sectors):
            o_ref[i, s, :, :FS] = x_ref[i, :, s * FS : (s + 1) * FS]
            nxt = ((s + 1) % sectors) * FS
            prv = ((s - 1) % sectors) * FS + FS - LANES
            o_ref[i, s, :, FS:] = jnp.where(
                low, x_ref[i, :, nxt : nxt + LANES], x_ref[i, :, prv : prv + LANES]
            )
        stores[i].start()
    for store in stores:
        store.wait()


def pack(fine, sectors):
    rows, columns, width = fine.shape
    return pl.pallas_call(
        pack_kernel,
        out_shape=jax.ShapeDtypeStruct((sectors, rows, columns, FS + LANES), BF),
        in_specs=[pl.BlockSpec(memory_space=pl.ANY)],
        out_specs=pl.BlockSpec(memory_space=pl.ANY),
        scratch_shapes=[
            pltpu.VMEM((rows, columns, width), BF),
            pltpu.VMEM((rows, sectors, columns, FS + LANES), BF),
            pltpu.SemaphoreType.DMA((rows,)),
            pltpu.SemaphoreType.DMA((rows,)),
        ],
        compiler_params=params(8),
        name="pack",
    )(fine)


def rotate_sum(values, first, position, cos_ref, sin_ref, row):
    real = imag = None
    for j in range(KIDS):
        p = position[first + j]
        c = cos_ref[pl.ds(p, 1), :]
        s = sin_ref[pl.ds(p, 1), :]
        u = values[(row + j) * 32 : (row + j) * 32 + 16]
        v = values[(row + j) * 32 + 16 : (row + j) * 32 + 32]
        re = c * u - s * v
        im = s * u + c * v
        real = re if real is None else real + re
        imag = im if imag is None else imag + im
    return real, imag


def swap(tile):
    return pltpu.roll(tile, HALO, axis=1)


GROUP = 4


def fine_kernel(child, position, slot, x_hbm, w_ref, cos_ref, sin_ref, o_ref, *rest):
    lhs, sem = rest[-2:]
    halos = rest[:-2]
    mids, rows, _ = o_ref.shape
    per = GROUP * KIDS
    groups = mids // GROUP
    span = per * rows

    def fetch(g, _):
        for i in range(per):
            pltpu.make_async_copy(
                x_hbm.at[child[g * per + i]], lhs.at[g * per + i], sem.at[g]
            ).start()
        return 0

    lax.fori_loop(0, groups, fetch, 0)
    low = low_lanes((rows // 2, LANES))

    def body(g, _):
        base = g * per
        pltpu.make_async_copy(x_hbm.at[pl.ds(0, per)], lhs.at[pl.ds(base, per)], sem.at[g]).wait()
        block = lhs[pl.ds(base, per)].reshape(span, lhs.shape[2])
        values = jnp.dot(block, w_ref[...], preferred_element_type=F32)
        for m in range(GROUP):
            real, imag = rotate_sum(
                values, base + m * KIDS, position, cos_ref, sin_ref, m * KIDS
            )
            at = slot[g * GROUP + m]
            o_ref[at, :16] = real.astype(BF)
            o_ref[at, 16:] = imag.astype(BF)
            if halos:
                head, tail = real[:, :LANES], imag[:, :LANES]
                halos[0][at] = jnp.where(low, head, swap(tail)).astype(BF)
                head, tail = real[:, LANES:], imag[:, LANES:]
                halos[1][at] = jnp.where(low, swap(head), tail).astype(BF)
        return 0

    lax.fori_loop(0, groups, body, 0)


def lift_fine(child, position, slot, x, w, cos, sin, with_halos):
    boxes, rows, k = x.shape
    mids = boxes // KIDS
    n = w.shape[1]
    whole = lambda shape: pl.BlockSpec(shape, lambda i, *_: (0,) * len(shape))
    shapes = [(mids, rows, n)] + [(mids, rows // 2, LANES)] * (2 if with_halos else 0)
    return pl.pallas_call(
        fine_kernel,
        out_shape=[jax.ShapeDtypeStruct(shape, BF) for shape in shapes],
        grid_spec=pltpu.PrefetchScalarGridSpec(
            num_scalar_prefetch=3,
            grid=(1,),
            in_specs=[
                pl.BlockSpec(memory_space=pl.ANY),
                whole((k, n)),
                whole(cos.shape),
                whole(sin.shape),
            ],
            out_specs=[whole(shape) for shape in shapes],
            scratch_shapes=[
                pltpu.VMEM((boxes, rows, k), BF),
                pltpu.SemaphoreType.DMA((mids // GROUP,)),
            ],
        ),
        compiler_params=params(14),
        cost_estimate=pl.CostEstimate(
            flops=2 * boxes * rows * k * n, bytes_accessed=2 * boxes * rows * k, transcendentals=0
        ),
        name="lift_fine",
    )(child, position, slot, x, w, cos, sin)


def mid_kernel(position, e_ref, c_ref, n_ref, p_ref, w_ref, cos_ref, sin_ref, o_ref, lhs):
    boxes, rows, _ = e_ref.shape
    half = rows // 2
    edge = 2 * LANES
    inner = c_ref.shape[2]

    @pl.when(pl.program_id(0) == 0)
    def _():
        low = low_lanes((half, LANES))
        lhs[:, :edge] = e_ref[...].reshape(boxes * rows, edge)
        lhs[:, edge : edge + inner] = c_ref[...].reshape(boxes * rows, inner)
        for m in range(boxes):
            nxt = n_ref[m].astype(F32)
            prv = p_ref[m].astype(F32)
            real = jnp.where(low, nxt, swap(prv))
            imag = jnp.where(low, swap(nxt), prv)
            lhs[m * rows : m * rows + half, edge + inner :] = real.astype(BF)
            lhs[m * rows + half : (m + 1) * rows, edge + inner :] = imag.astype(BF)

    values = jnp.dot(lhs[...], w_ref[...], preferred_element_type=F32)
    for t in range(boxes // KIDS):
        real, imag = rotate_sum(values, t * KIDS, position, cos_ref, sin_ref, t * KIDS)
        o_ref[t, :16] = real.astype(BF)
        o_ref[t, 16:] = imag.astype(BF)


def lift_mid(position, edges, central, from_next, from_prev, w, cos, sin, first, tiles):
    boxes, rows, _ = edges.shape
    k = w.shape[0]
    whole = lambda a: pl.BlockSpec(a.shape, lambda i, *_: (0,) * a.ndim)
    return pl.pallas_call(
        mid_kernel,
        out_shape=jax.ShapeDtypeStruct((boxes // KIDS, rows, tiles * TILE), BF),
        grid_spec=pltpu.PrefetchScalarGridSpec(
            num_scalar_prefetch=1,
            grid=(tiles,),
            in_specs=[
                whole(edges),
                whole(central),
                whole(from_next),
                whole(from_prev),
                pl.BlockSpec((k, TILE), lambda i, *_: (0, i + first)),
                pl.BlockSpec((cos.shape[0], TILE), lambda i, *_: (0, i + first)),
                pl.BlockSpec((sin.shape[0], TILE), lambda i, *_: (0, i + first)),
            ],
            out_specs=pl.BlockSpec((boxes // KIDS, rows, TILE), lambda i, *_: (0, 0, i)),
            scratch_shapes=[pltpu.VMEM((boxes * rows, k), BF)],
        ),
        compiler_params=params(14),
        cost_estimate=pl.CostEstimate(
            flops=2 * boxes * rows * k * tiles * TILE,
            bytes_accessed=2 * k * tiles * TILE,
            transcendentals=0,
        ),
        name="lift_mid",
    )(position, edges, central, from_next, from_prev, w, cos, sin)


def accumulate(t, starts, source, kind, held, op_ref, initial):
    def pairs(i, carry):
        real, imag = carry
        for n in range(UNROLL):
            at = i * UNROLL + n
            u = source[at]
            k = kind[at]
            xr = held[u, :16].astype(F32)
            xi = held[u, 16:].astype(F32)
            tr = op_ref[k, 0:1, :]
            ti = op_ref[k, 1:2, :]
            real = real + tr * xr - ti * xi
            imag = imag + tr * xi + ti * xr
        return real, imag

    return lax.fori_loop(starts[t], starts[t + 1], pairs, initial)


def near_kernel(starts, source, kind, a_ref, b_ref, op_ref, o_ref, held):
    size = a_ref.shape[0]
    held[:size] = a_ref[...]
    held[size:] = b_ref[...]

    def target(t, _):
        zero = jnp.zeros((16, held.shape[2]), F32)
        real, imag = accumulate(t, starts, source, kind, held, op_ref, (zero, zero))
        o_ref[t, 0] = real
        o_ref[t, 1] = imag
        return 0

    lax.fori_loop(0, size, target, 0)


def translate_near(lists, own, core, operators, first, tiles):
    size, rows, _ = own.shape
    part = pl.BlockSpec((size, rows, TILE), lambda i, *_: (0, 0, i))
    return pl.pallas_call(
        near_kernel,
        out_shape=jax.ShapeDtypeStruct((size, 2, rows // 2, tiles * TILE), F32),
        grid_spec=pltpu.PrefetchScalarGridSpec(
            num_scalar_prefetch=3,
            grid=(tiles,),
            in_specs=[
                part,
                part,
                pl.BlockSpec(operators.shape[:2] + (TILE,), lambda i, *_: (0, 0, i + first)),
            ],
            out_specs=pl.BlockSpec((size, 2, rows // 2, TILE), lambda i, *_: (0, 0, 0, i)),
            scratch_shapes=[pltpu.VMEM((2 * size, rows, TILE), BF)],
        ),
        compiler_params=params(6),
        cost_estimate=pl.CostEstimate(
            flops=2 * size * rows * 512 * tiles * TILE // 8,
            bytes_accessed=16 * size * rows * tiles * TILE,
            transcendentals=0,
        ),
        name="translate_near",
    )(*lists, own, core, operators)


def far_kernel(
    starts, source, kind, child, position, a_ref, b_ref, near_ref, op_ref, cos_ref, sin_ref, *rest
):
    top_ref, spread_ref, held = rest[-3:]
    size = a_ref.shape[0]
    held[:size] = a_ref[...]
    held[size:] = b_ref[...]

    def target(t, _):
        real, imag = accumulate(
            t, starts, source, kind, held, op_ref, (near_ref[t, 0], near_ref[t, 1])
        )
        top_ref[t, 0] = real
        top_ref[t, 1] = imag
        real = real.astype(BF).astype(F32)
        imag = imag.astype(BF).astype(F32)
        for j in range(KIDS):
            m = child[t * KIDS + j]
            p = position[t * KIDS + j]
            c = cos_ref[pl.ds(p, 1), :]
            s = sin_ref[pl.ds(p, 1), :]
            spread_ref[m, :16] = (c * real + s * imag).astype(BF)
            spread_ref[m, 16:] = (c * imag - s * real).astype(BF)
        return 0

    lax.fori_loop(0, size, target, 0)


def translate_far(lists, child, position, far, both, near, operators, cos, sin, held, first, tiles):
    size, rows, _ = far.shape
    mids = size * KIDS
    width = cos.shape[1]
    part = pl.BlockSpec((size, rows, TILE), lambda i, *_: (0, 0, i))
    wide = lambda a: pl.BlockSpec((a.shape[0], TILE), lambda i, *_: (0, i + first))
    extra = [] if held is None else [held]
    return pl.pallas_call(
        far_kernel,
        out_shape=(
            jax.ShapeDtypeStruct((size, 2, rows // 2, width), F32),
            jax.ShapeDtypeStruct((mids, rows, tiles * TILE), BF),
        ),
        grid_spec=pltpu.PrefetchScalarGridSpec(
            num_scalar_prefetch=5,
            grid=(tiles,),
            in_specs=[
                part,
                part,
                pl.BlockSpec((size, 2, rows // 2, TILE), lambda i, *_: (0, 0, 0, i)),
                pl.BlockSpec(operators.shape[:2] + (TILE,), lambda i, *_: (0, 0, i + first)),
                wide(cos),
                wide(sin),
            ]
            + [pl.BlockSpec(memory_space=pl.ANY)] * len(extra),
            out_specs=(
                pl.BlockSpec((size, 2, rows // 2, TILE), lambda i, *_: (0, 0, 0, i + first)),
                pl.BlockSpec((mids, rows, TILE), lambda i, *_: (0, 0, i)),
            ),
            scratch_shapes=[pltpu.VMEM((2 * size, rows, TILE), BF)],
        ),
        input_output_aliases={} if held is None else {11: 0},
        compiler_params=params(8),
        cost_estimate=pl.CostEstimate(
            flops=2 * size * rows * 512 * tiles * TILE // 8,
            bytes_accessed=16 * size * rows * tiles * TILE,
            transcendentals=0,
        ),
        name="translate_far",
    )(*lists, child, position, far, both, near, operators, cos, sin, *extra)


def halo_kernel(x_ref, w_ref, before_ref, up_ref, down_ref):
    boxes, rows, _ = x_ref.shape
    half = rows // 2
    low = low_lanes((half, LANES))
    values = lax.dot_general(
        x_ref[...].reshape(boxes * rows, x_ref.shape[2]),
        w_ref[...],
        (((1,), (1,)), ((), ())),
        preferred_element_type=F32,
    )
    for m in range(boxes):
        real = values[m * rows : m * rows + half] + before_ref[m, :half]
        imag = values[m * rows + half : (m + 1) * rows] + before_ref[m, half:]
        up_ref[m] = jnp.where(low, real, swap(imag)).astype(BF)
        down_ref[m] = jnp.where(low, swap(real), imag).astype(BF)


def halo_out(spread, w, before):
    boxes, rows, _ = spread.shape
    shape = jax.ShapeDtypeStruct((boxes, rows // 2, LANES), BF)
    return pl.pallas_call(
        halo_kernel,
        out_shape=(shape, shape),
        compiler_params=params(8),
        name="halo_out",
    )(spread, w, before)


def edge_kernel(x_ref, p_ref, n_ref, o_ref):
    boxes, rows, _ = x_ref.shape
    half = rows // 2
    low = low_lanes((half, LANES))

    def add(from_prev):
        for m in range(boxes):
            halo = (p_ref if from_prev else n_ref)[m].astype(F32)
            turned = swap(halo)
            real, imag = (halo, turned) if from_prev else (turned, halo)
            keep = low == from_prev
            o_ref[m, :half] = x_ref[m, :half] + jnp.where(keep, real, 0.0)
            o_ref[m, half:] = x_ref[m, half:] + jnp.where(keep, imag, 0.0)

    @pl.when(pl.program_id(0) == 0)
    def _():
        add(True)

    @pl.when(pl.program_id(0) == 1)
    def _():
        add(False)


def add_edges(central, from_prev, from_next):
    boxes, rows, width = central.shape
    last = width // LANES - 1
    tile = pl.BlockSpec((boxes, rows, LANES), lambda i: (0, 0, i * last))
    halo = pl.BlockSpec((boxes, rows // 2, LANES), lambda i: (0, 0, 0))
    return pl.pallas_call(
        edge_kernel,
        out_shape=jax.ShapeDtypeStruct(central.shape, F32),
        grid=(2,),
        in_specs=[tile, halo, halo],
        out_specs=tile,
        input_output_aliases={0: 0},
        compiler_params=params(4),
        name="add_edges",
    )(central, from_prev, from_next)


def children_of(parents, positions):
    n = parents.shape[0]
    index = jnp.arange(n, dtype=jnp.int32)
    before = (parents[None, :] < parents[:, None]) | (
        (parents[None, :] == parents[:, None]) & (index[None, :] < index[:, None])
    )
    rank = jnp.sum(before.astype(jnp.int32), axis=1)
    match = (rank[None, :] == index[:, None]).astype(jnp.int32)
    return (
        jnp.sum(match * index[None, :], axis=1),
        jnp.sum(match * positions[None, :], axis=1),
        rank,
    )


def pair_lists(target, source, kind, take, base, count, kinds):
    pairs = target.shape[0]
    index = jnp.arange(pairs, dtype=jnp.int32)
    local = jnp.where(take, target - base, -1)
    boxes = jnp.arange(count, dtype=jnp.int32)
    mine = local[None, :] == boxes[:, None]
    padded = (jnp.sum(mine.astype(jnp.int32), axis=1) + UNROLL - 1) // UNROLL
    starts = jnp.sum(
        jnp.where(
            boxes[None, :] < jnp.arange(count + 1, dtype=jnp.int32)[:, None], padded[None, :], 0
        ),
        axis=1,
    )
    earlier = (local[None, :] == local[:, None]) & (index[None, :] < index[:, None])
    within = jnp.sum(earlier.astype(jnp.int32), axis=1)
    begin = jnp.sum(jnp.where(mine, starts[:count, None] * UNROLL, 0), axis=0)
    slot = jnp.where(jnp.any(mine, axis=0), begin + within, -1)
    slots = pairs + count * (UNROLL - 1)
    match = (slot[None, :] == jnp.arange(slots, dtype=jnp.int32)[:, None]).astype(jnp.int32)
    return (
        starts,
        jnp.sum(match * source[None, :], axis=1),
        kinds + jnp.sum(match * (kind - kinds)[None, :], axis=1),
    )


def per_device(
    fine_pattern,
    fine_interp,
    mid_interp,
    fine_angle,
    top_angle,
    translator,
    fine_position,
    mid_position,
    fine_parent,
    mid_parent,
    pair_target,
    pair_source,
    pair_kind,
):
    box = lax.axis_index("box")
    dirs = lax.axis_size("dir")
    fine_local, _, columns, width = fine_pattern.shape
    rows = 2 * columns
    fine_group = fine_local * dirs
    mid_group = fine_group // KIDS
    top_group = mid_group // KIDS
    kinds = translator.shape[0]
    up = [(i, (i + 1) % dirs) for i in range(dirs)]
    down = [((i + 1) % dirs, i) for i in range(dirs)]

    packed = pack(fine_pattern.reshape(fine_local * 2, columns, width), dirs)
    arrived = lax.all_to_all(packed, "dir", split_axis=0, concat_axis=0, tiled=True)
    arrived = arrived.reshape(fine_group, rows, FS + LANES)

    cut = lambda a, n: lax.dynamic_slice_in_dim(a, box * n, n)
    fine_child, fine_pos, _ = children_of(
        cut(fine_parent, fine_group), cut(fine_position, fine_group)
    )
    mid_child, mid_pos, mid_slot = children_of(
        cut(mid_parent, mid_group), cut(mid_position, mid_group)
    )
    away = (pair_source // top_group) ^ box
    slot = (away & 1) * top_group + pair_source % top_group
    near_lists = pair_lists(
        pair_target, slot, pair_kind, away < 2, box * top_group, top_group, kinds
    )
    far_lists = pair_lists(
        pair_target, slot, pair_kind, away >= 2, box * top_group, top_group, kinds
    )
    fine_cos, fine_sin = jnp.cos(fine_angle), jnp.sin(fine_angle)
    top_cos, top_sin = jnp.cos(top_angle), jnp.sin(top_angle)
    operators = jnp.concatenate(
        [translator.astype(F32), jnp.zeros((8,) + translator.shape[1:], F32)], axis=0
    )
    wf = fine_interp[0]
    wf = jnp.concatenate([wf[HALO : HALO + FS], wf[HALO + FS :], wf[:HALO]], axis=0)
    wm = mid_interp[0]
    last = HALO + MS - LANES
    wm_halo = jnp.concatenate([wm[HALO + MS :], wm[:HALO]], axis=0)
    wm_central = wm[HALO : HALO + MS]
    wm_up = jnp.concatenate(
        [wm[HALO : HALO + LANES], wm[last : HALO + MS], wm[HALO + LANES : last], wm_halo], axis=0
    )
    ends = lambda a: jnp.concatenate([a[:, :LANES], a[:, MS - LANES :]], axis=1)
    inside = lambda a: a[:, LANES : MS - LANES]

    edges, head, tail = lift_fine(
        fine_child, fine_pos, mid_slot, arrived, ends(wf), ends(fine_cos), ends(fine_sin), True
    )
    from_next = lax.ppermute(head, "dir", down)
    from_prev = lax.ppermute(tail, "dir", up)
    (central,) = lift_fine(
        fine_child, fine_pos, mid_slot, arrived, inside(wf), inside(fine_cos), inside(fine_sin),
        False,
    )
    core = [(i, i ^ 1) for i in range(4)]
    opposite = [(i, i ^ 2) for i in range(4)]
    far, both, near = [], [], []
    firsts = [sum(CHUNKS[:c]) for c in range(len(CHUNKS))]
    for c, tiles in enumerate(CHUNKS):
        own = lift_mid(
            mid_pos, edges, central, from_next, from_prev, wm_up, top_cos, top_sin,
            firsts[c], tiles,
        )
        far.append(lax.ppermute(own, "box", opposite))
        beside = lax.ppermute(own, "box", core)
        both.append(lax.ppermute(far[-1], "box", core))
        near.append(translate_near(near_lists, own, beside, operators, firsts[c], tiles))
    top_incoming = None
    middle = jnp.zeros((mid_group, rows, MS), F32)
    outer = jnp.zeros((mid_group, rows, LANES), F32)
    for c, tiles in enumerate(CHUNKS):
        top_incoming, spread = translate_far(
            far_lists, mid_child, mid_pos, far[c], both[c], near[c], operators, top_cos,
            top_sin, top_incoming, firsts[c], tiles,
        )
        at = slice(firsts[c] * TILE, (firsts[c] + tiles) * TILE)
        if c + 1 < len(CHUNKS):
            outer += jnp.einsum("bxn,kn->bxk", spread, wm_halo[:, at], preferred_element_type=F32)
        else:
            to_next, to_prev = halo_out(spread, wm_halo[:, at], outer)
            below = lax.ppermute(to_next, "dir", up)
            above = lax.ppermute(to_prev, "dir", down)
        middle += jnp.einsum("bxn,kn->bxk", spread, wm_central[:, at], preferred_element_type=F32)
    mid_incoming = add_edges(middle, below, above)
    return top_incoming, mid_incoming.reshape(mid_group, 2, columns, MS)


def solution(mesh):
    placed = (
        P(("box", "dir"), None, None, None),
        P("dir", None, None),
        P("dir", None, None),
        P(None, "dir"),
        P(None, "dir"),
        P(None, None, "dir"),
        P(),
        P(),
        P(),
        P(),
        P(),
        P(),
        P(),
    )

    return jax.shard_map(
        per_device,
        mesh=mesh,
        in_specs=placed,
        out_specs=(P("box", None, None, "dir"), P("box", None, None, "dir")),
        check_vma=False,
    )
```

time: 191 us -> 168 us (0.88)
  waiting for transfers between devices: 54 us -> 44.4 us
  local copies, waits for them, and re-layouts: 26.3 us -> 18.8 us
  starting transfers between devices: 28.7 us -> 35.4 us
  other arithmetic: 8.36 us -> 3.9 us
  matrix products: 15.6 us -> 11.6 us
  Pallas kernels: 55.4 us -> 52.2 us
    ppermute x7 -> x16, waiting for transfers between devices: 35.4 us -> 21.4 us  [the longest x4 19.3 us: per_device(): far.append(lax.ppermute(own, 'box', opposite))]
    ppermute x7 -> x16, starting transfers between devices: 19.3 us -> 25.9 us  [the longest x4 6.45 us: per_device(): far.append(lax.ppermute(own, 'box', opposite))]
    all_to_all x1, waiting for transfers between devices: 18.6 us -> 23 us  [per_device(): lax.all_to_all(packed, 'dir', split_axis=0, concat_axis=0, tiled=True)]
    dot_general x2 -> x7, matrix products: 15.6 us -> 11.6 us  [the longest x4 9.78 us: per_device(): jnp.einsum('bxn,kn->bxk', spread, wm_central[:, at], preferred_element_ty...]
    pallas_call x1, Pallas kernels: 5.93 us -> 1.98 us  [pack(): pl.pallas_call(pack_kernel, out_shape=jax.ShapeDtypeStruct((sectors, rows...]
    unnamed x42 -> x36, local copies, waits for them, and re-layouts: 16.2 us -> 12.8 us
    pallas_call x3 -> x11, Pallas kernels: 31.6 us -> 34.6 us  [the longest x4 14 us: translate_far(): pl.pallas_call(far_kernel, out_shape=(jax.ShapeDtypeStruct((size, 2, rows...]
    pallas_call x1 -> x4, Pallas kernels: 15.5 us -> 13.5 us  [lift_mid(): pl.pallas_call(mid_kernel, out_shape=jax.ShapeDtypeStruct((boxes // KIDS,...]
  transfers between devices with their start and end apart: 8 -> 17, of which waited for: 3 -> 4; matrix products, arithmetic and copies ran while one was open for 20% -> 16% of each run, Pallas kernels for 4% -> 22%
where the time goes in v2:
time: 168 us; the launch traced here: 167 us
  Pallas kernels  52.2 us (31%)
  waiting for transfers between devices  44.4 us (26%)
  starting transfers between devices  35.4 us (21%)
  local copies, waits for them, and re-layouts  18.8 us (11%)
  matrix products  11.6 us (7%)
  other arithmetic  3.9 us (2%)
    all_to_all x1, waiting for transfers between devices, per_device(): lax.all_to_all(packed, 'dir', split_axis=0, concat_axis=0, tiled=True)  23 us
    ppermute x4, waiting for transfers between devices, per_device(): far.append(lax.ppermute(own, 'box', opposite))  19.3 us
    pallas_call x4, Pallas kernels, translate_far(): pl.pallas_call(far_kernel, out_shape=(jax.ShapeDtypeStruct((size, 2, rows...  14 us
    pallas_call x4, Pallas kernels, lift_mid(): pl.pallas_call(mid_kernel, out_shape=jax.ShapeDtypeStruct((boxes // KIDS,...  13.5 us
    unnamed x36, local copies, waits for them, and re-layouts  12.8 us
    pallas_call x2, Pallas kernels, lift_fine(): pl.pallas_call(fine_kernel, out_shape=[jax.ShapeDtypeStruct(shape, BF) fo...  10.4 us
    dot_general x4, matrix products, per_device(): jnp.einsum('bxn,kn->bxk', spread, wm_central[:, at], preferred_element_ty...  9.78 us
    pallas_call x4, Pallas kernels, translate_near(): pl.pallas_call(near_kernel, out_shape=jax.ShapeDtypeStruct((size, 2, rows...  9.47 us
  transfers between devices with their start and end apart: 17, of which 4 were waited for; matrix products, arithmetic and copies ran while one was open for 16% of the time, Pallas kernels for 22%

profile of v2, /device:TPU:1, one launch (start us, length us, event | category | flops | bytes accessed | tf_op | source)
XLA Modules:
  0.0 167.4 jit_solution(2079509181977714043)
XLA Ops:
  0.6 1.6 copy-done.2
  2.2 2.0 %pack.1 = bf16[32,8,16,384]{3,2,1,0:T(8,128)(2,1)} custom-call(bf16[8,16,8192]{2,1,0:T(8,128)(2,1)S(1)} %bitcast.55), custom_call_target="tpu_custom_call" | custom-call | tf_op jit(solution)/shard_map/pack/pallas_call | solution.py:55
  4.3 9.5 %all-to-all-start = ((bf16[32,8,16,384]{3,2,1,0:T(8,128)(2,1)}), bf16[32,8,16,384]{3,2,1,0:T(8,128)(2,1)}, u32[]{:S(2)}, u32[]{:S(2)}) async-start(bf16[32,8,16,384]{3,2,1,0:T(8,128)(2,1)} %pack.1), calls=%async_computation | async-start | bytes 6291456 | tf_op jit(solution)/shard_map/all_to_all | solution.py:489
  14.7 0.8 dynamic_slice.15
  15.4 0.8 dynamic_slice.14
  16.9 2.1 %pad_convert_fusion.op_ref = f32[72,2,3328]{2,1,0:T(2,128)S(1)} fusion(bf16[64,2,3328]{2,1,0:T(2,128)(2,1)} %param.18), kind=kLoop, calls=%fused_computation.11 | loop fusion | flops 479232 | bytes 2768896 | tf_op jit(solution)/shard_map/concatenate | solution.py:509
  19.0 1.2 bitcast_dynamic-update-slice_fusion.2
  20.2 1.2 bitcast_dynamic-update-slice_fusion.1
  21.5 2.6 %bitcast_dynamic-update-slice_fusion = bf16[1024,3328]{1,0:T(8,128)(2,1)S(1)} fusion(bf16[1024,3328]{1,0:T(8,128)(2,1)S(1)} %bitcast_dynamic-update-slice_fusion.1, bf16[1,1024,3328]{2,1,0:T(8,128)(2,1)} %param.15), kind=kLoop, calls=%fused_computation.1 | loop fusion | bytes 8519680
  24.5 2.8 %copy-done = bf16[1024,3328]{1,0:T(8,128)(2,1)} copy-done((bf16[1024,3328]{1,0:T(8,128)(2,1)}, bf16[1024,3328]{1,0:T(8,128)(2,1)S(1)}, u32[]{:S(2)}) %copy-start) | copy-done | bytes 6815768
  28.1 0.8 slice_bitcast_fusion.13
  28.9 2.9 %slice_bitcast_fusion = bf16[896,3328]{1,0:T(8,128)(2,1)} fusion(bf16[1,1024,3328]{2,1,0:T(8,128)(2,1)S(1)} %bitcast.57), kind=kLoop, calls=%fused_computation | loop fusion | bytes 11927552 | tf_op jit(solution)/shard_map/slice | solution.py:517
  31.8 23.0 %all-to-all-done = bf16[32,8,16,384]{3,2,1,0:T(8,128)(2,1)} async-done(((bf16[32,8,16,384]{3,2,1,0:T(8,128)(2,1)}), bf16[32,8,16,384]{3,2,1,0:T(8,128)(2,1)}, u32[]{:S(2)}, u32[]{:S(2)}) %all-to-all-start) | async-done | bytes 3145760 | tf_op jit(solution)/shard_map/all_to_all | solution.py:489
  54.7 4.5 %lift_fine.2 = (bf16[32,32,256]{2,1,0:T(8,128)(2,1)S(1)}, bf16[32,16,128]{2,1,0:T(8,128)(2,1)S(1)}, bf16[32,16,128]{2,1,0:T(8,128)(2,1)S(1)}) custom-call(s32[128]{0:T(128)S(1)} %get-tuple-element.33.child, s32[128]{0:T(128)S(1)} %get-tuple-element.32.position, s32[32]{0:T(128)S(1)} %convert_reduce_fusion.3.slot, bf16[128,32,384]{2,1,0:T(8,128)(2,1)} %bitcast.1.x_hbm, ...), custom_call_target="tpu_custom_call" | custom-call | flops 805306368 | bytes 3145728 | tf_op jit(solution)/shard_map/lift_fine/pallas_call | solution.py:139
  59.3 5.6 %collective-permute-start = (bf16[32,16,128]{2,1,0:T(8,128)(2,1)S(1)}, bf16[32,16,128]{2,1,0:T(8,128)(2,1)S(1)}, u32[]{:S(2)}, u32[]{:S(2)}) collective-permute-start(bf16[32,16,128]{2,1,0:T(8,128)(2,1)S(1)} %get-tuple-element.16), channel_id=1, source_target_pairs={{1,0},{2,1},{3,2},{4,3},{5,4},{6,5},{7,6},{8,7},{9,8},{10,9},{11,1... | collective-permute-start | bytes 393224 | tf_op jit(solution)/shard_map/ppermute | solution.py:527
  64.8 5.9 %lift_fine.3.c_ref = bf16[32,32,640]{2,1,0:T(8,128)(2,1)S(1)} custom-call(s32[128]{0:T(128)S(1)} %get-tuple-element.33.child, s32[128]{0:T(128)S(1)} %get-tuple-element.32.position, s32[32]{0:T(128)S(1)} %convert_reduce_fusion.3.slot, bf16[128,32,384]{2,1,0:T(8,128)(2,1)} %bitcast.1.x_hbm, bf16[384,640]{1,0:T(8,128)(2,1)S(1)} %pad_maximum_fusion.w_ref, ...), custom_call_target="tpu_custom_call" | custom-call | flops 2013265920 | bytes 3145728 | tf_op jit(solution)/shard_map/lift_fine/pallas_call | solution.py:139
  70.8 2.1 %collective-permute-done.1.p_ref = bf16[32,16,128]{2,1,0:T(8,128)(2,1)S(1)} collective-permute-done((bf16[32,16,128]{2,1,0:T(8,128)(2,1)S(1)}, bf16[32,16,128]{2,1,0:T(8,128)(2,1)S(1)}, u32[]{:S(2)}, u32[]{:S(2)}) %collective-permute-start.1) | collective-permute-done | bytes 131104 | tf_op jit(solution)/shard_map/ppermute | solution.py:528
  72.9 2.9 %copy-done.1 = bf16[1024,3328]{1,0:T(8,128)(2,1)S(1)} copy-done((bf16[1024,3328]{1,0:T(8,128)(2,1)S(1)}, bf16[1024,3328]{1,0:T(8,128)(2,1)}, u32[]{:S(2)}) %copy-start.1) | copy-done | bytes 6815768
  75.8 2.4 %lift_mid.7.a_ref = bf16[8,32,512]{2,1,0:T(8,128)(2,1)S(1)} custom-call(s32[32]{0:T(128)S(1)} %get-tuple-element.34.position, bf16[32,32,256]{2,1,0:T(8,128)(2,1)S(1)} %get-tuple-element.15.e_ref, bf16[32,32,640]{2,1,0:T(8,128)(2,1)S(1)} %lift_fine.3.c_ref, bf16[32,16,128]{2,1,0:T(8,128)(2,1)S(1)} %collective-permute-done.n_ref, ...), custom_call_target="tpu_custom_call" | custom-call | flops 1073741824 | bytes 1048576 | tf_op jit(solution)/shard_map/lift_mid/pallas_call | solution.py:195
  78.2 2.3 %collective-permute-start.13 = (bf16[8,32,512]{2,1,0:T(8,128)(2,1)S(1)}, bf16[8,32,512]{2,1,0:T(8,128)(2,1)S(1)}, u32[]{:S(2)}, u32[]{:S(2)}) collective-permute-start(bf16[8,32,512]{2,1,0:T(8,128)(2,1)S(1)} %lift_mid.7.a_ref), channel_id=1, source_target_pairs={{0,32},{32,0},{64,96},{96,64},{1,33},{33,1},{65,97},{97,65},{2,34}... | collective-permute-start | bytes 786440 | tf_op jit(solution)/shard_map/ppermute | solution.py:543
  80.5 3.3 %collective-permute-start.11 = (bf16[8,32,512]{2,1,0:T(8,128)(2,1)S(1)}, bf16[8,32,512]{2,1,0:T(8,128)(2,1)S(1)}, u32[]{:S(2)}, u32[]{:S(2)}) collective-permute-start(bf16[8,32,512]{2,1,0:T(8,128)(2,1)S(1)} %lift_mid.7.a_ref), channel_id=1, source_target_pairs={{0,64},{32,96},{64,0},{96,32},{1,65},{33,97},{65,1},{97,33},{2,66}... | collective-permute-start | bytes 786440 | tf_op jit(solution)/shard_map/ppermute | solution.py:542
  83.8 3.2 %lift_mid.4.a_ref = bf16[8,32,768]{2,1,0:T(8,128)(2,1)S(1)} custom-call(s32[32]{0:T(128)S(1)} %get-tuple-element.34.position, bf16[32,32,256]{2,1,0:T(8,128)(2,1)S(1)} %get-tuple-element.15.e_ref, bf16[32,32,640]{2,1,0:T(8,128)(2,1)S(1)} %lift_fine.3.c_ref, bf16[32,16,128]{2,1,0:T(8,128)(2,1)S(1)} %collective-permute-done.n_ref, ...), custom_call_target="tpu_custom_call" | custom-call | flops 1610612736 | bytes 1572864 | tf_op jit(solution)/shard_map/lift_mid/pallas_call | solution.py:195
  87.4 4.0 %lift_mid.5.a_ref = bf16[8,32,1024]{2,1,0:T(8,128)(2,1)S(1)} custom-call(s32[32]{0:T(128)S(1)} %get-tuple-element.34.position, bf16[32,32,256]{2,1,0:T(8,128)(2,1)S(1)} %get-tuple-element.15.e_ref, bf16[32,32,640]{2,1,0:T(8,128)(2,1)S(1)} %lift_fine.3.c_ref, bf16[32,16,128]{2,1,0:T(8,128)(2,1)S(1)} %collective-permute-done.n_ref, ...), custom_call_target="tpu_custom_call" | custom-call | flops 2147483648 | bytes 2097152 | tf_op jit(solution)/shard_map/lift_mid/pallas_call | solution.py:195
  91.4 3.0 %collective-permute-start.5 = (bf16[8,32,1024]{2,1,0:T(8,128)(2,1)S(1)}, bf16[8,32,1024]{2,1,0:T(8,128)(2,1)S(1)}, u32[]{:S(2)}, u32[]{:S(2)}) collective-permute-start(bf16[8,32,1024]{2,1,0:T(8,128)(2,1)S(1)} %lift_mid.5.a_ref), channel_id=1, source_target_pairs={{0,64},{32,96},{64,0},{96,32},{1,65},{33,97},{65,1},{97,33},{2,66}... | collective-permute-start | bytes 1572872 | tf_op jit(solution)/shard_map/ppermute | solution.py:542
  94.4 4.0 %lift_mid.6.a_ref = bf16[8,32,1024]{2,1,0:T(8,128)(2,1)S(1)} custom-call(s32[32]{0:T(128)S(1)} %get-tuple-element.34.position, bf16[32,32,256]{2,1,0:T(8,128)(2,1)S(1)} %get-tuple-element.15.e_ref, bf16[32,32,640]{2,1,0:T(8,128)(2,1)S(1)} %lift_fine.3.c_ref, bf16[32,16,128]{2,1,0:T(8,128)(2,1)S(1)} %collective-permute-done.n_ref, ...), custom_call_target="tpu_custom_call" | custom-call | flops 2147483648 | bytes 2097152 | tf_op jit(solution)/shard_map/lift_mid/pallas_call | solution.py:195
  98.9 1.0 collective-permute-start.7
  100.0 1.0 collective-permute-start.12
  101.0 9.6 %collective-permute-done.5.a_ref = bf16[8,32,1024]{2,1,0:T(8,128)(2,1)S(1)} collective-permute-done((bf16[8,32,1024]{2,1,0:T(8,128)(2,1)S(1)}, bf16[8,32,1024]{2,1,0:T(8,128)(2,1)S(1)}, u32[]{:S(2)}, u32[]{:S(2)}) %collective-permute-start.5) | collective-permute-done | bytes 524320 | tf_op jit(solution)/shard_map/ppermute | solution.py:542
  110.7 1.6 collective-permute-start.6
  112.3 9.6 %collective-permute-done.8.a_ref = bf16[8,32,1024]{2,1,0:T(8,128)(2,1)S(1)} collective-permute-done((bf16[8,32,1024]{2,1,0:T(8,128)(2,1)S(1)}, bf16[8,32,1024]{2,1,0:T(8,128)(2,1)S(1)}, u32[]{:S(2)}, u32[]{:S(2)}) %collective-permute-start.8) | collective-permute-done | bytes 524320 | tf_op jit(solution)/shard_map/ppermute | solution.py:542
  121.9 1.0 collective-permute-start.9
  122.9 1.7 translate_near.7.near_ref
  124.6 2.2 %translate_near.4.near_ref = f32[8,2,16,768]{3,2,1,0:T(8,128)S(1)} custom-call(s32[9]{0:T(128)S(1)} %select_reduce_fusion.10.starts, s32[280]{0:T(512)S(1)} %get-tuple-element.31.source, s32[280]{0:T(512)S(1)} %broadcast_add_fusion.kind, bf16[8,32,768]{2,1,0:T(8,128)(2,1)S(1)} %lift_mid.4.a_ref, bf16[8,32,768]{2,1,0:T(8,128)(2,1)S(1)} %collective-permute-done.4.b_ref, ...), custom_call_target="tpu_custom_call" | custom-call | flops 25165824 | bytes 3145728 | tf_op jit(solution)/shard_map/translate_near/pallas_call | solution.py:259
  127.5 2.6 %translate_far.4 = (f32[8,2,16,3328]{3,2,1,0:T(8,128)}, bf16[32,32,512]{2,1,0:T(8,128)(2,1)S(1)}) custom-call(s32[9]{0:T(128)S(1)} %select_reduce_fusion.11.starts, s32[280]{0:T(512)S(1)} %get-tuple-element.30.source, s32[280]{0:T(512)S(1)} %broadcast_add_fusion.1.kind, s32[32]{0:T(128)S(1)} %get-tuple-element.35.child, s32[32]{0:T(128)S(1)} %get-tuple-element.34.position, ...), custom_call_target="tpu_custom_call" | custom-call | flops 16777216 | bytes 2097152 | tf_op jit(solution)/shard_map/translate_far/pallas_call | solution.py:318
  130.1 2.8 %translate_near.5.near_ref = f32[8,2,16,1024]{3,2,1,0:T(8,128)S(1)} custom-call(s32[9]{0:T(128)S(1)} %select_reduce_fusion.10.starts, s32[280]{0:T(512)S(1)} %get-tuple-element.31.source, s32[280]{0:T(512)S(1)} %broadcast_add_fusion.kind, bf16[8,32,1024]{2,1,0:T(8,128)(2,1)S(1)} %lift_mid.5.a_ref, bf16[8,32,1024]{2,1,0:T(8,128)(2,1)S(1)} %collective-permute-done.7.b_ref, ...), custom_call_target="tpu_custom_call" | custom-call | flops 33554432 | bytes 4194304 | tf_op jit(solution)/shard_map/translate_near/pallas_call | solution.py:259
  132.9 2.8 %translate_near.6.near_ref = f32[8,2,16,1024]{3,2,1,0:T(8,128)S(1)} custom-call(s32[9]{0:T(128)S(1)} %select_reduce_fusion.10.starts, s32[280]{0:T(512)S(1)} %get-tuple-element.31.source, s32[280]{0:T(512)S(1)} %broadcast_add_fusion.kind, bf16[8,32,1024]{2,1,0:T(8,128)(2,1)S(1)} %lift_mid.6.a_ref, bf16[8,32,1024]{2,1,0:T(8,128)(2,1)S(1)} %collective-permute-done.10.b_ref, ...), custom_call_target="tpu_custom_call" | custom-call | flops 33554432 | bytes 4194304 | tf_op jit(solution)/shard_map/translate_near/pallas_call | solution.py:259
  135.7 1.3 fusion.4
  137.0 4.1 %translate_far.5 = (f32[8,2,16,3328]{3,2,1,0:T(8,128)}, bf16[32,32,1024]{2,1,0:T(8,128)(2,1)S(1)}) custom-call(s32[9]{0:T(128)S(1)} %select_reduce_fusion.11.starts, s32[280]{0:T(512)S(1)} %get-tuple-element.30.source, s32[280]{0:T(512)S(1)} %broadcast_add_fusion.1.kind, s32[32]{0:T(128)S(1)} %get-tuple-element.35.child, ...), custom_call_target="tpu_custom_call", output_to_operand_aliasing={{0}: (11, {})} | custom-call | flops 33554432 | bytes 4194304 | tf_op jit(solution)/shard_map/translate_far/pallas_call | solution.py:318
  141.1 4.1 %translate_far.6 = (f32[8,2,16,3328]{3,2,1,0:T(8,128)}, bf16[32,32,1024]{2,1,0:T(8,128)(2,1)S(1)}) custom-call(s32[9]{0:T(128)S(1)} %select_reduce_fusion.11.starts, s32[280]{0:T(512)S(1)} %get-tuple-element.30.source, s32[280]{0:T(512)S(1)} %broadcast_add_fusion.1.kind, s32[32]{0:T(128)S(1)} %get-tuple-element.35.child, ...), custom_call_target="tpu_custom_call", output_to_operand_aliasing={{0}: (11, {})} | custom-call | flops 33554432 | bytes 4194304 | tf_op jit(solution)/shard_map/translate_far/pallas_call | solution.py:318
  145.2 0.7 fusion.12
  145.9 2.4 %fusion = f32[32,32,896]{2,1,0:T(8,128)S(1)} fusion(bf16[32,32,1024]{2,1,0:T(8,128)(2,1)S(1)} %get-tuple-element.24, bf16[896,3328]{1,0:T(8,128)(2,1)S(1)} %bitcast.60), kind=kOutput, calls=%fused_computation.4 | convolution fusion | flops 1879048192 | bytes 7602176 | tf_op jit(solution)/shard_map/bxn,kn->bxk/dot_general | solution.py:561
  148.2 2.4 %fusion.1 = f32[32,32,896]{2,1,0:T(8,128)S(1)} fusion(bf16[32,32,1024]{2,1,0:T(8,128)(2,1)S(1)} %get-tuple-element.23, bf16[896,3328]{1,0:T(8,128)(2,1)S(1)} %bitcast.60), kind=kOutput, calls=%fused_computation.6 | convolution fusion | flops 1879048192 | bytes 7602176 | tf_op jit(solution)/shard_map/bxn,kn->bxk/dot_general | solution.py:561
  150.6 0.7 fusion.15
  151.8 3.3 %translate_far.7 = (f32[8,2,16,3328]{3,2,1,0:T(8,128)}, bf16[32,32,768]{2,1,0:T(8,128)(2,1)S(1)}) custom-call(s32[9]{0:T(128)S(1)} %select_reduce_fusion.11.starts, s32[280]{0:T(512)S(1)} %get-tuple-element.30.source, s32[280]{0:T(512)S(1)} %broadcast_add_fusion.1.kind, s32[32]{0:T(128)S(1)} %get-tuple-element.35.child, ...), custom_call_target="tpu_custom_call", output_to_operand_aliasing={{0}: (11, {})} | custom-call | flops 25165824 | bytes 3145728 | tf_op jit(solution)/shard_map/translate_far/pallas_call | solution.py:318
  155.1 0.7 halo_out.1
  155.8 5.7 %collective-permute-start.15 = (bf16[32,16,128]{2,1,0:T(8,128)(2,1)S(1)}, bf16[32,16,128]{2,1,0:T(8,128)(2,1)S(1)}, u32[]{:S(2)}, u32[]{:S(2)}) collective-permute-start(bf16[32,16,128]{2,1,0:T(8,128)(2,1)S(1)} %get-tuple-element.27), channel_id=1, source_target_pairs={{1,0},{2,1},{3,2},{4,3},{5,4},{6,5},{7,6},{8,7},{9,8},{10,9},{11,1... | collective-permute-start | bytes 393224 | tf_op jit(solution)/shard_map/ppermute | solution.py:560
  161.5 3.8 %add_add_fusion.x_ref = f32[32,32,896]{2,1,0:T(8,128)} fusion(f32[32,32,896]{2,1,0:T(8,128)S(1)} %fusion, f32[32,32,896]{2,1,0:T(8,128)S(1)} %fusion.4, f32[32,32,896]{2,1,0:T(8,128)S(1)} %fusion.1, bf16[32,32,768]{2,1,0:T(8,128)(2,1)S(1)} %get-tuple-element.25.x_ref, bf16[896,3328]{1,0:T(8,128)(2,1)S(1)} %bitcast.60), kind=kOutput, calls=%fused_computation.2 | convolution fusion | flops 1412038656 | bytes 17629184 | tf_op jit(solution)/shard_map/bxn,kn->bxk/dot_general | solution.py:561
  165.2 2.1 %add_edges.1 = f32[32,32,896]{2,1,0:T(8,128)} custom-call(f32[32,32,896]{2,1,0:T(8,128)} %add_add_fusion.x_ref, bf16[32,16,128]{2,1,0:T(8,128)(2,1)S(1)} %collective-permute-done.14.p_ref, bf16[32,16,128]{2,1,0:T(8,128)(2,1)S(1)} %collective-permute-done.15.n_ref), custom_call_target="tpu_custom_call", output_to_operand_aliasing={{}: (0, {})} | custom-call | tf_op jit(solution)/shard_map/add_edges/pallas_call | solution.py:409
  (91 shorter events, 4.9 us)
Async XLA Ops:
  0.6 1.6 copy-start.2
  4.2 9.6 %copy-start.7 = (s32[256]{0:T(256)S(1)}, s32[256]{0:T(256)}, u32[]{:S(2)}) copy-start(s32[256]{0:T(256)} %param.24) | copy-start | bytes 3076
  4.2 9.6 %copy-start.9 = (s32[256]{0:T(256)S(1)}, s32[256]{0:T(256)}, u32[]{:S(2)}) copy-start(s32[256]{0:T(256)} %param.23) | copy-start | bytes 3076
  4.2 10.1 %copy-start.6 = (f32[8,896]{1,0:T(8,128)S(1)}, f32[8,896]{1,0:T(8,128)}, u32[]{:S(2)}) copy-start(f32[8,896]{1,0:T(8,128)} %param.16) | copy-start | bytes 86020
  4.2 10.2 %copy-start.4 = (bf16[1,384,896]{2,1,0:T(8,128)(2,1)S(1)}, bf16[1,384,896]{2,1,0:T(8,128)(2,1)}, u32[]{:S(2)}) copy-start(bf16[1,384,896]{2,1,0:T(8,128)(2,1)} %param.14) | copy-start | bytes 2064388
  4.3 12.1 %copy-start.10 = (s32[128]{0:T(128)S(1)}, s32[128]{0:T(128)}, u32[]{:S(2)}) copy-start(s32[128]{0:T(128)} %param.20) | copy-start | bytes 1540
  4.3 12.2 %copy-start.11 = (s32[128]{0:T(128)S(1)}, s32[128]{0:T(128)}, u32[]{:S(2)}) copy-start(s32[128]{0:T(128)} %param.22) | copy-start | bytes 1540
  4.3 50.4 %all-to-all-start = ((bf16[32,8,16,384]{3,2,1,0:T(8,128)(2,1)}), bf16[32,8,16,384]{3,2,1,0:T(8,128)(2,1)}, u32[]{:S(2)}, u32[]{:S(2)}) async-start(bf16[32,8,16,384]{3,2,1,0:T(8,128)(2,1)} %pack.1), calls=%async_computation | async-start | bytes 6291456 | tf_op jit(solution)/shard_map/all_to_all | solution.py:489
  16.9 7.2 %slice-start = ((s8[6815744]{0:T(1024)(128)(4,1)}), s8[4194304]{0:T(1024)(128)(4,1)S(1)}, s32[]{:S(2)}) async-start(s8[6815744]{0:T(1024)(128)(4,1)} %bitcast.56), calls=%async_computation.1 | async-start | bytes 8388608
  21.4 3.0 %slice-start.1 = ((s8[6815744]{0:T(1024)(128)(4,1)}), s8[2621440]{0:T(1024)(128)(4,1)S(1)}, s32[]{:S(2)}) async-start(s8[6815744]{0:T(1024)(128)(4,1)} %bitcast.56), calls=%async_computation.2 | async-start | bytes 5242880
  21.4 6.2 %copy-start.5 = (f32[8,3328]{1,0:T(8,128)S(1)}, f32[8,3328]{1,0:T(8,128)}, u32[]{:S(2)}) copy-start(f32[8,3328]{1,0:T(8,128)} %param.17) | copy-start | bytes 319492
  24.5 2.8 %copy-start = (bf16[1024,3328]{1,0:T(8,128)(2,1)}, bf16[1024,3328]{1,0:T(8,128)(2,1)S(1)}, u32[]{:S(2)}) copy-start(bf16[1024,3328]{1,0:T(8,128)(2,1)S(1)} %constant_dynamic-update-slice_fusion.w_ref) | copy-start | bytes 20447236
  59.3 11.5 %collective-permute-start = (bf16[32,16,128]{2,1,0:T(8,128)(2,1)S(1)}, bf16[32,16,128]{2,1,0:T(8,128)(2,1)S(1)}, u32[]{:S(2)}, u32[]{:S(2)}) collective-permute-start(bf16[32,16,128]{2,1,0:T(8,128)(2,1)S(1)} %get-tuple-element.16), channel_id=1, source_target_pairs={{1,0},{2,1},{3,2},{4,3},{5,4},{6,5},{7,6},{8,7},{9,8},{10,9},{11,1... | collective-permute-start | bytes 393224 | tf_op jit(solution)/shard_map/ppermute | solution.py:527
  64.8 8.0 %collective-permute-start.1 = (bf16[32,16,128]{2,1,0:T(8,128)(2,1)S(1)}, bf16[32,16,128]{2,1,0:T(8,128)(2,1)S(1)}, u32[]{:S(2)}, u32[]{:S(2)}) collective-permute-start(bf16[32,16,128]{2,1,0:T(8,128)(2,1)S(1)} %get-tuple-element.17), channel_id=1, source_target_pairs={{0,1},{1,2},{2,3},{3,4},{4,5},{5,6},{6,7},{7,8},{8,9},{9,10},{10,1... | collective-permute-start | bytes 393224 | tf_op jit(solution)/shard_map/ppermute | solution.py:528
  72.9 2.9 %copy-start.1 = (bf16[1024,3328]{1,0:T(8,128)(2,1)S(1)}, bf16[1024,3328]{1,0:T(8,128)(2,1)}, u32[]{:S(2)}) copy-start(bf16[1024,3328]{1,0:T(8,128)(2,1)} %copy-done) | copy-start | bytes 20447236
  78.2 20.2 %collective-permute-start.13 = (bf16[8,32,512]{2,1,0:T(8,128)(2,1)S(1)}, bf16[8,32,512]{2,1,0:T(8,128)(2,1)S(1)}, u32[]{:S(2)}, u32[]{:S(2)}) collective-permute-start(bf16[8,32,512]{2,1,0:T(8,128)(2,1)S(1)} %lift_mid.7.a_ref), channel_id=1, source_target_pairs={{0,32},{32,0},{64,96},{96,64},{1,33},{33,1},{65,97},{97,65},{2,34}... | collective-permute-start | bytes 786440 | tf_op jit(solution)/shard_map/ppermute | solution.py:543
  80.5 18.4 %collective-permute-start.11 = (bf16[8,32,512]{2,1,0:T(8,128)(2,1)S(1)}, bf16[8,32,512]{2,1,0:T(8,128)(2,1)S(1)}, u32[]{:S(2)}, u32[]{:S(2)}) collective-permute-start(bf16[8,32,512]{2,1,0:T(8,128)(2,1)S(1)} %lift_mid.7.a_ref), channel_id=1, source_target_pairs={{0,64},{32,96},{64,0},{96,32},{1,65},{33,97},{65,1},{97,33},{2,66}... | collective-permute-start | bytes 786440 | tf_op jit(solution)/shard_map/ppermute | solution.py:542
  86.9 12.9 %collective-permute-start.4 = (bf16[8,32,768]{2,1,0:T(8,128)(2,1)S(1)}, bf16[8,32,768]{2,1,0:T(8,128)(2,1)S(1)}, u32[]{:S(2)}, u32[]{:S(2)}) collective-permute-start(bf16[8,32,768]{2,1,0:T(8,128)(2,1)S(1)} %lift_mid.4.a_ref), channel_id=1, source_target_pairs={{0,32},{32,0},{64,96},{96,64},{1,33},{33,1},{65,97},{97,65},{2,34}... | collective-permute-start | bytes 1179656 | tf_op jit(solution)/shard_map/ppermute | solution.py:543
  87.4 12.6 %collective-permute-start.2 = (bf16[8,32,768]{2,1,0:T(8,128)(2,1)S(1)}, bf16[8,32,768]{2,1,0:T(8,128)(2,1)S(1)}, u32[]{:S(2)}, u32[]{:S(2)}) collective-permute-start(bf16[8,32,768]{2,1,0:T(8,128)(2,1)S(1)} %lift_mid.4.a_ref), channel_id=1, source_target_pairs={{0,64},{32,96},{64,0},{96,32},{1,65},{33,97},{65,1},{97,33},{2,66}... | collective-permute-start | bytes 1179656 | tf_op jit(solution)/shard_map/ppermute | solution.py:542
  91.4 7.1 %copy-start.8 = (s32[256]{0:T(256)S(1)}, s32[256]{0:T(256)}, u32[]{:S(2)}) copy-start(s32[256]{0:T(256)} %param.25) | copy-start | bytes 3076
  91.4 31.5 %copy-start.3 = (bf16[64,3328]{1,0:T(8,128)(2,1)S(1)}, bf16[64,3328]{1,0:T(8,128)(2,1)}, u32[]{:S(2)}) copy-start(bf16[64,3328]{1,0:T(8,128)(2,1)} %get-tuple-element.39) | copy-start | bytes 1277956
  91.4 19.3 %collective-permute-start.5 = (bf16[8,32,1024]{2,1,0:T(8,128)(2,1)S(1)}, bf16[8,32,1024]{2,1,0:T(8,128)(2,1)S(1)}, u32[]{:S(2)}, u32[]{:S(2)}) collective-permute-start(bf16[8,32,1024]{2,1,0:T(8,128)(2,1)S(1)} %lift_mid.5.a_ref), channel_id=1, source_target_pairs={{0,64},{32,96},{64,0},{96,32},{1,65},{33,97},{65,1},{97,33},{2,66}... | collective-permute-start | bytes 1572872 | tf_op jit(solution)/shard_map/ppermute | solution.py:542
  98.4 23.5 %collective-permute-start.8 = (bf16[8,32,1024]{2,1,0:T(8,128)(2,1)S(1)}, bf16[8,32,1024]{2,1,0:T(8,128)(2,1)S(1)}, u32[]{:S(2)}, u32[]{:S(2)}) collective-permute-start(bf16[8,32,1024]{2,1,0:T(8,128)(2,1)S(1)} %lift_mid.6.a_ref), channel_id=1, source_target_pairs={{0,64},{32,96},{64,0},{96,32},{1,65},{33,97},{65,1},{97,33},{2,66}... | collective-permute-start | bytes 1572872 | tf_op jit(solution)/shard_map/ppermute | solution.py:542
  98.9 31.2 %collective-permute-start.7 = (bf16[8,32,1024]{2,1,0:T(8,128)(2,1)S(1)}, bf16[8,32,1024]{2,1,0:T(8,128)(2,1)S(1)}, u32[]{:S(2)}, u32[]{:S(2)}) collective-permute-start(bf16[8,32,1024]{2,1,0:T(8,128)(2,1)S(1)} %lift_mid.5.a_ref), channel_id=1, source_target_pairs={{0,32},{32,0},{64,96},{96,64},{1,33},{33,1},{65,97},{97,65},{2,34}... | collective-permute-start | bytes 1572872 | tf_op jit(solution)/shard_map/ppermute | solution.py:543
  99.9 33.0 %collective-permute-start.10 = (bf16[8,32,1024]{2,1,0:T(8,128)(2,1)S(1)}, bf16[8,32,1024]{2,1,0:T(8,128)(2,1)S(1)}, u32[]{:S(2)}, u32[]{:S(2)}) collective-permute-start(bf16[8,32,1024]{2,1,0:T(8,128)(2,1)S(1)} %lift_mid.6.a_ref), channel_id=1, source_target_pairs={{0,32},{32,0},{64,96},{96,64},{1,33},{33,1},{65,97},{97,65},{2,34}... | collective-permute-start | bytes 1572872 | tf_op jit(solution)/shard_map/ppermute | solution.py:543
  100.0 26.8 %collective-permute-start.12 = (bf16[8,32,512]{2,1,0:T(8,128)(2,1)S(1)}, bf16[8,32,512]{2,1,0:T(8,128)(2,1)S(1)}, u32[]{:S(2)}, u32[]{:S(2)}) collective-permute-start(bf16[8,32,512]{2,1,0:T(8,128)(2,1)S(1)} %collective-permute-done.11.a_ref), channel_id=1, source_target_pairs={{0,32},{32,0},{64,96},{96,64},{1,33},{33,1},{65,97},{97,65},{2,34}... | collective-permute-start | bytes 786440 | tf_op jit(solution)/shard_map/ppermute | solution.py:544
  110.7 30.4 %collective-permute-start.6 = (bf16[8,32,1024]{2,1,0:T(8,128)(2,1)S(1)}, bf16[8,32,1024]{2,1,0:T(8,128)(2,1)S(1)}, u32[]{:S(2)}, u32[]{:S(2)}) collective-permute-start(bf16[8,32,1024]{2,1,0:T(8,128)(2,1)S(1)} %collective-permute-done.5.a_ref), channel_id=1, source_target_pairs={{0,32},{32,0},{64,96},{96,64},{1,33},{33,1},{65,97},{97,65},{2,34}... | collective-permute-start | bytes 1572872 | tf_op jit(solution)/shard_map/ppermute | solution.py:544
  121.9 15.1 %collective-permute-start.9 = (bf16[8,32,1024]{2,1,0:T(8,128)(2,1)S(1)}, bf16[8,32,1024]{2,1,0:T(8,128)(2,1)S(1)}, u32[]{:S(2)}, u32[]{:S(2)}) collective-permute-start(bf16[8,32,1024]{2,1,0:T(8,128)(2,1)S(1)} %collective-permute-done.8.a_ref), channel_id=1, source_target_pairs={{0,32},{32,0},{64,96},{96,64},{1,33},{33,1},{65,97},{97,65},{2,34}... | collective-permute-start | bytes 1572872 | tf_op jit(solution)/shard_map/ppermute | solution.py:544
  126.8 24.9 %collective-permute-start.3 = (bf16[8,32,768]{2,1,0:T(8,128)(2,1)S(1)}, bf16[8,32,768]{2,1,0:T(8,128)(2,1)S(1)}, u32[]{:S(2)}, u32[]{:S(2)}) collective-permute-start(bf16[8,32,768]{2,1,0:T(8,128)(2,1)S(1)} %collective-permute-done.2.a_ref), channel_id=1, source_target_pairs={{0,32},{32,0},{64,96},{96,64},{1,33},{33,1},{65,97},{97,65},{2,34}... | collective-permute-start | bytes 1179656 | tf_op jit(solution)/shard_map/ppermute | solution.py:544
  127.5 8.2 %slice-start.2 = ((s8[5963776]{0:T(1024)(128)(4,1)}), s8[4194304]{0:T(1024)(128)(4,1)S(1)}, s32[]{:S(2)}) async-start(s8[5963776]{0:T(1024)(128)(4,1)} %bitcast.59), calls=%async_computation.3 | async-start | bytes 8388608
  130.1 5.6 %slice-start.3 = ((s8[5963776]{0:T(1024)(128)(4,1)}), s8[1769472]{0:T(1024)(128)(4,1)S(1)}, s32[]{:S(2)}) async-start(s8[5963776]{0:T(1024)(128)(4,1)} %bitcast.59), calls=%async_computation.4 | async-start | bytes 3538944
  155.7 9.5 %collective-permute-start.14 = (bf16[32,16,128]{2,1,0:T(8,128)(2,1)S(1)}, bf16[32,16,128]{2,1,0:T(8,128)(2,1)S(1)}, u32[]{:S(2)}, u32[]{:S(2)}) collective-permute-start(bf16[32,16,128]{2,1,0:T(8,128)(2,1)S(1)} %get-tuple-element.26), channel_id=1, source_target_pairs={{0,1},{1,2},{2,3},{3,4},{4,5},{5,6},{6,7},{7,8},{8,9},{9,10},{10,1... | collective-permute-start | bytes 393224 | tf_op jit(solution)/shard_map/ppermute | solution.py:559
  155.8 9.4 %collective-permute-start.15 = (bf16[32,16,128]{2,1,0:T(8,128)(2,1)S(1)}, bf16[32,16,128]{2,1,0:T(8,128)(2,1)S(1)}, u32[]{:S(2)}, u32[]{:S(2)}) collective-permute-start(bf16[32,16,128]{2,1,0:T(8,128)(2,1)S(1)} %get-tuple-element.27), channel_id=1, source_target_pairs={{1,0},{2,1},{3,2},{4,3},{5,4},{6,5},{7,6},{8,7},{9,8},{10,9},{11,1... | collective-permute-start | bytes 393224 | tf_op jit(solution)/shard_map/ppermute | solution.py:560
